TPU v7x, 128 devices: a whole 4x4x4 slice. The times are simulated.
128 devices in a mesh: seq: 32 (over x, y, core), tp: 4 (over z).
Axes of the slice: x: 4, y: 4, z: 4, core: 2. Of those that a mesh axis runs over, the one named last changes fastest.
Arguments:
- token_ids: int32 [64, 4], replicated, may hold values from 0 to 51199
- embedding: bfloat16 [51200, 2048], P(('seq', 'tp')), may hold values from -8 to 8
- group_of: int32 [64], replicated, may hold values from 0 to 7, as said below
- prefix_len: int32 [8], replicated, may hold values from 1 to 2048, as said below
- tail_len: int32 [64], replicated, may hold values from 1 to 512, as said below
- block_map: int32 [512, 2], P('seq'), may hold values from -1 to 71, as said below
- k_cache: bfloat16 [2, 65536, 2048], P(None, 'seq', 'tp'), may hold values from -100 to 100
- v_cache: bfloat16 [2, 65536, 2048], P(None, 'seq', 'tp'), may hold values from -12 to 12
- ln_gain: float32 [2, 2048], replicated, may hold values from 0.25 to 1.75
- ln_bias: float32 [2, 2048], replicated, may hold values from -1.5 to 1.5
- w_qkv: bfloat16 [2, 2048, 3, 2048], P(None, 'seq', None, 'tp'), may hold values from -0.125 to 0.125
- w_fc1: bfloat16 [2, 2048, 8192], P(None, 'seq', 'tp'), may hold values from -0.125 to 0.125
- b_fc1: float32 [2, 8192], P(None, 'tp'), may hold values from -2.5 to 2.5
- w_out: bfloat16 [2, 2048, 2048], P(None, ('tp', 'seq')), may hold values from -0.125 to 0.125
- w_fc2: bfloat16 [2, 8192, 2048], P(None, ('tp', 'seq')), may hold values from -0.0625 to 0.0625
Outputs:
- hidden_out: float32 [64, 4, 2048], replicated
Inputs may be any that keep to these rules, and one draw needn't show every extreme that they name: `group_of`: every group holds exactly 8 requests. `prefix_len`: some group's prompt is 2048 long. `tail_len`: some request's tail is 512 long. `block_map`: row b gives the segment held by cache block b (slots b * 128 to b * 128 + 127): g for group g's prompt, 8 + r for request r's tail, -1 for none; and its rank within the segment. A segment of length L holds ranks 0 to ceil(L / 128) - 1, each in exactly one block; a block with segment -1 has rank 0.
All inputs are finite; a program needn't handle non-finite values.
Results may differ from a plain program's by a relative error of at most 0.04.
The roundings to bfloat16 on the way count: a program that leaves them out, or rounds other values in their place, can miss the bound.
Values may be sent and summed in bfloat16 or wider, within the bound.
A program may use at most 192 MiB of HBM per device.

v0:
```python
import functools
import math

import jax
import numpy as np
import jax.numpy as jnp
from jax import lax
from jax.experimental import pallas as pl
from jax.experimental.pallas import tpu as pltpu
from jax.sharding import PartitionSpec as P

HEADS = 32
HEAD_DIM = 64
ROT = 32
LAYERS = 2
BLOCK = 128
SPAN = 512
MESH_IDS = pl.DeviceIdType.MESH

very_negative = -1e30


def layer_norm(values, gain_row, bias_row):
    average = jnp.mean(values, axis=-1, keepdims=True)
    centred = values - average
    variance = jnp.mean(centred * centred, axis=-1, keepdims=True)
    return centred * lax.rsqrt(variance + 1e-05) * gain_row + bias_row


def rotary(values, positions):
    half_width = ROT // 2
    frequency = jnp.exp(
        jnp.arange(half_width, dtype=jnp.float32) * (-2.0 * math.log(10000.0) / ROT)
    )
    angles = positions.astype(jnp.float32)[:, None] * frequency[None, :]
    cosine = jnp.cos(angles)[:, None, :]
    sine_part = jnp.sin(angles)[:, None, :]
    low_half = values[..., :half_width]
    high_half = values[..., half_width:ROT]
    return jnp.concatenate(
        [
            low_half * cosine - high_half * sine_part,
            high_half * cosine + low_half * sine_part,
            values[..., ROT:],
        ],
        axis=-1,
    )


def _group_ids(whole, tp_count):
    seq_index = lax.axis_index("seq")
    tp_index = lax.axis_index("tp")
    if whole:
        me = seq_index * tp_count + tp_index

        def peer(j):
            return (j // tp_count, j % tp_count)

    else:
        me = seq_index

        def peer(j):
            return (j, tp_index)

    return me, peer


_KERNEL_IDS = {}


def _kernel_id(key):
    if key not in _KERNEL_IDS:
        _KERNEL_IDS[key] = len(_KERNEL_IDS)
    return _KERNEL_IDS[key]


def _enter(n, me, peer):
    barrier = pltpu.get_barrier_semaphore()

    def greet(i, carry):
        j = lax.rem(me + i, n)
        pl.semaphore_signal(barrier, 1, device_id=peer(j), device_id_type=MESH_IDS)
        return carry

    lax.fori_loop(1, n, greet, 0)
    pl.semaphore_wait(barrier, n - 1)


def _rcopy(src, dst, send_sem, recv_sem, device):
    return pltpu.make_async_remote_copy(
        src_ref=src,
        dst_ref=dst,
        send_sem=send_sem,
        recv_sem=recv_sem,
        device_id=device,
        device_id_type=MESH_IDS,
    )


def _allreduce_kernel(n, whole, tp_count, x_ref, o_ref, rs_buf, ag_buf, s1, r1, s2, r2):
    me, peer = _group_ids(whole, tp_count)
    _enter(n, me, peer)

    def start_scatter(i, carry):
        j = lax.rem(me + i, n)
        _rcopy(x_ref.at[j], rs_buf.at[me], s1.at[j], r1.at[me], peer(j)).start()
        return carry

    lax.fori_loop(1, n, start_scatter, 0)

    def gather_sum(i, acc):
        j = lax.rem(me + i, n)
        _rcopy(x_ref.at[j], rs_buf.at[j], s1.at[j], r1.at[j], peer(j)).wait_recv()
        return acc + rs_buf[j].astype(jnp.float32)

    total = lax.fori_loop(1, n, gather_sum, x_ref[me].astype(jnp.float32))
    ag_buf[me] = total.astype(ag_buf.dtype)

    def start_gather(i, carry):
        j = lax.rem(me + i, n)
        _rcopy(ag_buf.at[me], ag_buf.at[me], s2.at[j], r2.at[me], peer(j)).start()
        return carry

    lax.fori_loop(1, n, start_gather, 0)

    def finish(i, carry):
        j = lax.rem(me + i, n)
        _rcopy(ag_buf.at[j], ag_buf.at[j], s2.at[j], r2.at[j], peer(j)).wait_recv()
        _rcopy(x_ref.at[j], rs_buf.at[me], s1.at[j], r1.at[me], peer(j)).wait_send()
        _rcopy(ag_buf.at[me], ag_buf.at[me], s2.at[j], r2.at[me], peer(j)).wait_send()
        return carry

    lax.fori_loop(1, n, finish, 0)
    o_ref[...] = ag_buf[...]


def allreduce(x, whole, tp_count):
    n = x.shape[0]
    return pl.pallas_call(
        functools.partial(_allreduce_kernel, n, whole, tp_count),
        out_shape=jax.ShapeDtypeStruct(x.shape, x.dtype),
        in_specs=[pl.BlockSpec(memory_space=pltpu.VMEM)],
        out_specs=pl.BlockSpec(memory_space=pltpu.VMEM),
        scratch_shapes=[
            pltpu.VMEM(x.shape, x.dtype),
            pltpu.VMEM(x.shape, x.dtype),
            pltpu.SemaphoreType.DMA((n,)),
            pltpu.SemaphoreType.DMA((n,)),
            pltpu.SemaphoreType.DMA((n,)),
            pltpu.SemaphoreType.DMA((n,)),
        ],
        compiler_params=pltpu.CompilerParams(
            has_side_effects=True,
            collective_id=_kernel_id(("allreduce", whole, x.shape, str(x.dtype))),
        ),
    )(x)


def _allreduce_chip_kernel(tp_count, x_ref, o_ref, pbuf, sbuf, rs_buf, ag_buf, sa, ra, s1, r1, s2, r2, sd, rd):
    seq_index = lax.axis_index("seq")
    tp_index = lax.axis_index("tp")
    n = x_ref.shape[1]
    core = seq_index % 2
    other = 1 - core
    me = (seq_index // 2) * tp_count + tp_index
    partner = (seq_index + 1 - 2 * core, tp_index)

    def peer(j):
        return ((j // tp_count) * 2 + core, j % tp_count)

    barrier = pltpu.get_barrier_semaphore()

    def greet(i, carry):
        j = lax.rem(me + i, n)
        pl.semaphore_signal(barrier, 1, device_id=peer(j), device_id_type=MESH_IDS)
        return carry

    lax.fori_loop(1, n, greet, 0)
    pl.semaphore_signal(barrier, 1, device_id=partner, device_id_type=MESH_IDS)
    pl.semaphore_wait(barrier, n)
    _allreduce_chip_body(tp_count, x_ref, o_ref, pbuf, sbuf, rs_buf, ag_buf, sa, ra, s1, r1, s2, r2, sd, rd)


def _allreduce_chip_body(tp_count, x_ref, o_ref, pbuf, sbuf, rs_buf, ag_buf, sa, ra, s1, r1, s2, r2, sd, rd):
    seq_index = lax.axis_index("seq")
    tp_index = lax.axis_index("tp")
    n = x_ref.shape[1]
    core = seq_index % 2
    other = 1 - core
    me = (seq_index // 2) * tp_count + tp_index
    partner = (seq_index + 1 - 2 * core, tp_index)

    def peer(j):
        return ((j // tp_count) * 2 + core, j % tp_count)

    swap = _rcopy(x_ref.at[other], pbuf, sa, ra, partner)
    swap.start()
    swap.wait_recv()
    sbuf[...] = (x_ref[core].astype(jnp.float32) + pbuf[...].astype(jnp.float32)).astype(sbuf.dtype)

    def start_scatter(i, carry):
        j = lax.rem(me + i, n)
        _rcopy(sbuf.at[j], rs_buf.at[me], s1.at[j], r1.at[me], peer(j)).start()
        return carry

    lax.fori_loop(1, n, start_scatter, 0)

    def gather_sum(i, acc):
        j = lax.rem(me + i, n)
        _rcopy(sbuf.at[j], rs_buf.at[j], s1.at[j], r1.at[j], peer(j)).wait_recv()
        return acc + rs_buf[j].astype(jnp.float32)

    total = lax.fori_loop(1, n, gather_sum, sbuf[me].astype(jnp.float32))
    ag_buf[core, me] = total.astype(ag_buf.dtype)

    def start_gather(i, carry):
        j = lax.rem(me + i, n)
        _rcopy(ag_buf.at[core, me], ag_buf.at[core, me], s2.at[j], r2.at[me], peer(j)).start()
        return carry

    lax.fori_loop(1, n, start_gather, 0)

    def finish(i, carry):
        j = lax.rem(me + i, n)
        _rcopy(ag_buf.at[core, j], ag_buf.at[core, j], s2.at[j], r2.at[j], peer(j)).wait_recv()
        _rcopy(sbuf.at[j], rs_buf.at[me], s1.at[j], r1.at[me], peer(j)).wait_send()
        _rcopy(ag_buf.at[core, me], ag_buf.at[core, me], s2.at[j], r2.at[me], peer(j)).wait_send()
        return carry

    lax.fori_loop(1, n, finish, 0)
    swap.wait_send()
    back = _rcopy(ag_buf.at[core], ag_buf.at[core], sd, rd, partner)
    back.start()
    _rcopy(ag_buf.at[other], ag_buf.at[other], sd, rd, partner).wait_recv()
    back.wait_send()
    o_ref[...] = ag_buf[...]


def allreduce_chip(x, tp_count, sum_dtype=None):
    n = x.shape[1]
    half = x.shape[1:]
    sum_dtype = x.dtype if sum_dtype is None else sum_dtype
    return pl.pallas_call(
        functools.partial(_allreduce_chip_kernel, tp_count),
        out_shape=jax.ShapeDtypeStruct(x.shape, sum_dtype),
        in_specs=[pl.BlockSpec(memory_space=pltpu.VMEM)],
        out_specs=pl.BlockSpec(memory_space=pltpu.VMEM),
        scratch_shapes=[
            pltpu.VMEM(half, x.dtype),
            pltpu.VMEM(half, sum_dtype),
            pltpu.VMEM(half, sum_dtype),
            pltpu.VMEM(x.shape, sum_dtype),
            pltpu.SemaphoreType.DMA(()),
            pltpu.SemaphoreType.DMA(()),
            pltpu.SemaphoreType.DMA((n,)),
            pltpu.SemaphoreType.DMA((n,)),
            pltpu.SemaphoreType.DMA((n,)),
            pltpu.SemaphoreType.DMA((n,)),
            pltpu.SemaphoreType.DMA(()),
            pltpu.SemaphoreType.DMA(()),
        ],
        compiler_params=pltpu.CompilerParams(
            has_side_effects=True,
            collective_id=_kernel_id(("allreduce_chip", x.shape, str(x.dtype), str(sum_dtype))),
        ),
    )(x)


def _opening_kernel(tp_count, x_ref, w_ref, o_ref, wo_ref, pbuf, sbuf, rs_buf, ag_buf, sa, ra, s1, r1, s2, r2, sd, rd, wbuf, ws, wr):
    seq_index = lax.axis_index("seq")
    tp_index = lax.axis_index("tp")
    count = 2 * x_ref.shape[1]
    me_all = seq_index * tp_count + tp_index
    _enter(count, me_all, lambda j: (j // tp_count, j % tp_count))
    n = w_ref.shape[0]

    def start(i, carry):
        j = lax.rem(seq_index + i, n)
        _rcopy(w_ref.at[j], wbuf.at[seq_index], ws.at[j], wr.at[seq_index], (j, tp_index)).start()
        return carry

    lax.fori_loop(1, n, start, 0)
    _allreduce_chip_body(tp_count, x_ref, o_ref, pbuf, sbuf, rs_buf, ag_buf, sa, ra, s1, r1, s2, r2, sd, rd)

    def finish(i, carry):
        j = lax.rem(seq_index + i, n)
        _rcopy(w_ref.at[j], wbuf.at[j], ws.at[j], wr.at[j], (j, tp_index)).wait_recv()
        _rcopy(w_ref.at[j], wbuf.at[seq_index], ws.at[j], wr.at[seq_index], (j, tp_index)).wait_send()
        return carry

    lax.fori_loop(1, n, finish, 0)
    wbuf[seq_index] = w_ref[seq_index]
    wo_ref[...] = wbuf[...]


def opening(x, w, tp_count):
    n = x.shape[1]
    half = x.shape[1:]
    m = w.shape[0]
    return pl.pallas_call(
        functools.partial(_opening_kernel, tp_count),
        out_shape=(jax.ShapeDtypeStruct(x.shape, x.dtype), jax.ShapeDtypeStruct(w.shape, w.dtype)),
        in_specs=[pl.BlockSpec(memory_space=pltpu.VMEM)] * 2,
        out_specs=(pl.BlockSpec(memory_space=pltpu.VMEM), pl.BlockSpec(memory_space=pltpu.VMEM)),
        scratch_shapes=[
            pltpu.VMEM(half, x.dtype),
            pltpu.VMEM(half, x.dtype),
            pltpu.VMEM(half, x.dtype),
            pltpu.VMEM(x.shape, x.dtype),
            pltpu.SemaphoreType.DMA(()),
            pltpu.SemaphoreType.DMA(()),
            pltpu.SemaphoreType.DMA((n,)),
            pltpu.SemaphoreType.DMA((n,)),
            pltpu.SemaphoreType.DMA((n,)),
            pltpu.SemaphoreType.DMA((n,)),
            pltpu.SemaphoreType.DMA(()),
            pltpu.SemaphoreType.DMA(()),
            pltpu.VMEM(w.shape, w.dtype),
            pltpu.SemaphoreType.DMA((m,)),
            pltpu.SemaphoreType.DMA((m,)),
        ],
        compiler_params=pltpu.CompilerParams(
            has_side_effects=True,
            collective_id=_kernel_id(("opening", x.shape, w.shape)),
        ),
    )(x, w)


def _all_to_all_kernel(n, whole, tp_count, x_ref, o_ref, buf, s1, r1):
    me, peer = _group_ids(whole, tp_count)
    _enter(n, me, peer)

    def start(i, carry):
        j = lax.rem(me + i, n)
        _rcopy(x_ref.at[j], buf.at[me], s1.at[j], r1.at[me], peer(j)).start()
        return carry

    lax.fori_loop(1, n, start, 0)

    def finish(i, carry):
        j = lax.rem(me + i, n)
        _rcopy(x_ref.at[j], buf.at[j], s1.at[j], r1.at[j], peer(j)).wait_recv()
        _rcopy(x_ref.at[j], buf.at[me], s1.at[j], r1.at[me], peer(j)).wait_send()
        return carry

    lax.fori_loop(1, n, finish, 0)
    buf[me] = x_ref[me]
    o_ref[...] = buf[...]


def all_to_all(x, whole, tp_count):
    n = x.shape[0]
    return pl.pallas_call(
        functools.partial(_all_to_all_kernel, n, whole, tp_count),
        out_shape=jax.ShapeDtypeStruct(x.shape, x.dtype),
        in_specs=[pl.BlockSpec(memory_space=pltpu.VMEM)],
        out_specs=pl.BlockSpec(memory_space=pltpu.VMEM),
        scratch_shapes=[
            pltpu.VMEM(x.shape, x.dtype),
            pltpu.SemaphoreType.DMA((n,)),
            pltpu.SemaphoreType.DMA((n,)),
        ],
        compiler_params=pltpu.CompilerParams(
            has_side_effects=True,
            collective_id=_kernel_id(("all_to_all", whole, x.shape, str(x.dtype))),
        ),
    )(x)


def _attention_kernel(scale, q_ref, k_ref, v_ref, mask_ref, o_ref, m_ref, l_ref):
    valid = mask_ref[...] > 0.5
    scores = lax.dot_general(
        q_ref[0], k_ref[...], (((1,), (1,)), ((), ())), preferred_element_type=jnp.float32
    )
    scores = jnp.where(valid, scores * scale, very_negative)
    top = jnp.max(scores, axis=1, keepdims=True)
    weights = jnp.where(valid, jnp.exp(scores - top), 0.0)
    total = jnp.sum(weights, axis=1, keepdims=True)
    o_ref[0] = jnp.dot(weights.astype(jnp.bfloat16), v_ref[...], preferred_element_type=jnp.float32)
    m_ref[0] = jnp.broadcast_to(top, m_ref.shape[1:])
    l_ref[0] = jnp.broadcast_to(total, l_ref.shape[1:])


def cache_attention(q_pad, k_cache, v_cache, mask, layer_index, scale):
    heads, rows, lanes = q_pad.shape
    slots = k_cache.shape[1]
    per_block = lanes // HEAD_DIM
    out_spec = pl.BlockSpec((1, rows, lanes), lambda h: (h, 0, 0))
    return pl.pallas_call(
        functools.partial(_attention_kernel, scale),
        grid=(heads,),
        out_shape=[jax.ShapeDtypeStruct((heads, rows, lanes), jnp.float32)] * 3,
        in_specs=[
            pl.BlockSpec((1, rows, lanes), lambda h: (h, 0, 0)),
            pl.BlockSpec((None, slots, lanes), lambda h: (layer_index, 0, h // per_block)),
            pl.BlockSpec((None, slots, lanes), lambda h: (layer_index, 0, h // per_block)),
            pl.BlockSpec((rows, slots), lambda h: (0, 0)),
        ],
        out_specs=[out_spec] * 3,
    )(q_pad, k_cache, v_cache, mask)


def per_device(
    token_ids,
    embedding,
    group_of,
    prefix_len,
    tail_len,
    block_map,
    k_cache,
    v_cache,
    ln_gain,
    ln_bias,
    w_qkv,
    w_fc1,
    b_fc1,
    w_out,
    w_fc2,
):
    tp_count = lax.axis_size("tp")
    seq_count = lax.axis_size("seq")
    all_count = tp_count * seq_count
    seq_index = lax.axis_index("seq")
    tp_index = lax.axis_index("tp")
    requests = token_ids.shape[0]
    new_tokens = token_ids.shape[1]
    rows = requests * new_tokens
    groups = prefix_len.shape[0]
    heads_local = HEADS // tp_count
    width = embedding.shape[1]
    score_scale = 1.0 / math.sqrt(HEAD_DIM)

    vocab_rows = embedding.shape[0]
    first_row = (seq_index * tp_count + tp_index) * vocab_rows
    local_ids = token_ids.reshape(-1) - first_row
    inside = (local_ids >= 0) & (local_ids < vocab_rows)
    picked = jnp.take(embedding, jnp.clip(local_ids, 0, vocab_rows - 1), axis=0)
    picked = jnp.where(inside[:, None], picked, jnp.zeros_like(picked))

    group_hit = group_of[:, None] == jnp.arange(groups, dtype=jnp.int32)[None, :]
    shared_len = jnp.sum(jnp.where(group_hit, prefix_len[None, :], 0), axis=1)
    base_positions = shared_len + tail_len
    positions = (base_positions[:, None] + jnp.arange(new_tokens, dtype=jnp.int32)[None, :]).reshape(-1)
    seg_len = jnp.concatenate([prefix_len, tail_len])
    seg_count = seg_len.shape[0]
    blocks_local = block_map.shape[0]
    seg_blk = block_map[:, 0]
    rank_blk = block_map[:, 1]
    seg_hit = seg_blk[:, None] == jnp.arange(seg_count, dtype=jnp.int32)[None, :]
    len_blk = jnp.sum(jnp.where(seg_hit, seg_len[None, :], 0), axis=1)
    slot_positions = rank_blk[:, None] * BLOCK + jnp.arange(BLOCK, dtype=jnp.int32)[None, :]
    live_slot = ((seg_blk[:, None] >= 0) & (slot_positions < len_blk[:, None])).reshape(-1)
    seg_slot = jnp.broadcast_to(seg_blk[:, None], (blocks_local, BLOCK)).reshape(-1)
    own_tail = seg_slot[None, :] == (groups + jnp.arange(requests, dtype=jnp.int32))[:, None]
    own_prompt = seg_slot[None, :] == group_of[:, None]
    allowed = (own_tail | own_prompt) & live_slot[None, :]
    allowed = jnp.repeat(allowed, new_tokens, axis=0)
    mask_f = allowed.astype(jnp.float32)

    rows_local = w_qkv.shape[1]
    unit_count = w_fc2.shape[1]
    sub_width = w_out.shape[1]
    pieces = HEAD_DIM // sub_width
    my_head = seq_index // pieces
    my_piece = seq_index % pieces
    causal = (
        jnp.arange(new_tokens, dtype=jnp.int32)[None, :]
        <= jnp.arange(new_tokens, dtype=jnp.int32)[:, None]
    )

    half_rot = ROT // 2
    pair_width = 2 * sub_width
    qkv_t = w_qkv.transpose(2, 3, 0, 1).reshape(3, heads_local, HEAD_DIM, LAYERS * rows_local)
    q_t = qkv_t[0].reshape(heads_local, 1, HEAD_DIM // pair_width, 1, pair_width, LAYERS * rows_local)
    q_t = jnp.broadcast_to(
        q_t, (heads_local, 1, HEAD_DIM // pair_width, pieces // 2, pair_width, LAYERS * rows_local)
    )
    k_t = jnp.broadcast_to(
        qkv_t[1][:, None], (heads_local, pieces, HEAD_DIM, LAYERS * rows_local)
    )
    v_t = qkv_t[2].reshape(seq_count, sub_width, LAYERS * rows_local)
    f_t = w_fc1.transpose(2, 0, 1).reshape(seq_count, unit_count, LAYERS * rows_local)
    message = jnp.concatenate(
        [
            q_t.reshape(seq_count, pair_width, LAYERS * rows_local),
            k_t.reshape(seq_count, HEAD_DIM, LAYERS * rows_local),
            v_t,
            f_t,
        ],
        axis=1,
    )
    cols_mine = message.shape[1]
    start_states, got_w = opening(
        picked.reshape(2, all_count // 2, -1, 128),
        message,
        tp_count,
    )
    hidden_state = start_states.reshape(rows, width).astype(jnp.float32)
    w_mine = (
        got_w.reshape(seq_count, cols_mine, LAYERS, rows_local)
        .transpose(2, 1, 0, 3)
        .reshape(LAYERS, cols_mine, seq_count * rows_local)
    )
    q_end = pair_width
    k_end = q_end + HEAD_DIM
    v_end = k_end + sub_width
    angles = positions.astype(jnp.float32)[:, None] * jnp.exp(
        jnp.arange(half_rot, dtype=jnp.float32) * (-2.0 * math.log(10000.0) / ROT)
    )[None, :]
    cosine = jnp.cos(angles)
    sine_part = jnp.sin(angles)
    for layer_index in range(LAYERS):
        normed = layer_norm(hidden_state, ln_gain[layer_index], ln_bias[layer_index]).astype(
            jnp.bfloat16
        )
        local = jnp.einsum(
            "rc,kc->rk", normed, w_mine[layer_index], preferred_element_type=jnp.float32
        )
        q_pair = local[:, :q_end]
        low_half = q_pair[:, :half_rot]
        high_half = q_pair[:, half_rot:]
        q_rot = jnp.concatenate(
            [low_half * cosine - high_half * sine_part, high_half * cosine + low_half * sine_part],
            axis=1,
        )
        q_pair = jnp.where(my_piece < 2, q_rot, q_pair)
        q_piece = lax.dynamic_slice_in_dim(q_pair, (my_piece % 2) * sub_width, sub_width, 1)
        q_piece = q_piece.astype(jnp.bfloat16).T
        k_h = rotary(local[:, None, q_end:k_end], positions)[:, 0].astype(jnp.bfloat16)
        v_h = local[:, k_end:v_end].astype(jnp.bfloat16)
        pre_act = local[:, v_end:]
        pre_act = (
            pre_act
            + lax.dynamic_slice_in_dim(b_fc1[layer_index], seq_index * unit_count, unit_count, 0)[
                None, :
            ]
        )
        activated = jax.nn.gelu(pre_act, approximate=True).astype(jnp.bfloat16)
        q_all = all_to_all(jnp.broadcast_to(q_piece[None], (seq_count,) + q_piece.shape), False, tp_count)
        queries = (
            q_all.reshape(heads_local, pieces, sub_width, rows)
            .transpose(3, 0, 1, 2)
            .reshape(rows, heads_local, HEAD_DIM)
        )
        per_block = 128 // HEAD_DIM
        same_half = (
            jnp.arange(per_block, dtype=jnp.int32)[:, None]
            == jnp.arange(per_block, dtype=jnp.int32)[None, :]
        )
        q_pairs = queries.reshape(rows, heads_local // per_block, per_block, HEAD_DIM).transpose(1, 2, 0, 3)
        q_pad = jnp.where(
            same_half[None, :, None, :, None], q_pairs[:, :, :, None, :], jnp.zeros((), jnp.bfloat16)
        ).reshape(heads_local, rows, 128)
        out_pad, max_pad, sum_pad = cache_attention(
            q_pad, k_cache, v_cache, mask_f, layer_index, score_scale
        )
        part_out = jnp.sum(
            jnp.where(
                same_half[None, :, None, :, None],
                out_pad.reshape(heads_local // per_block, per_block, rows, per_block, HEAD_DIM),
                0.0,
            ),
            axis=3,
        ).reshape(heads_local, rows, HEAD_DIM)
        part_max = max_pad[:, :, 0]
        part_sum = sum_pad[:, :, 0]
        out_pieces = (
            part_out.reshape(heads_local, rows, pieces, sub_width)
            .transpose(0, 2, 3, 1)
            .reshape(heads_local * pieces, sub_width, rows)
        )
        max_rows = jnp.repeat(part_max, pieces, axis=0)[:, None, :]
        sum_rows = jnp.repeat(part_sum, pieces, axis=0)[:, None, :]
        pad_rows = jnp.zeros((heads_local * pieces, 6, rows), jnp.float32)
        message = jnp.concatenate([out_pieces, max_rows, sum_rows, pad_rows], axis=1)
        received = all_to_all(message, False, tp_count)
        got_out = received[:, :sub_width, :]
        got_max = received[:, sub_width, :]
        got_sum = received[:, sub_width + 1, :]

        q_h = lax.dynamic_index_in_dim(queries, my_head, 1, keepdims=False)
        q_h = q_h.reshape(requests, new_tokens, HEAD_DIM)
        k_h = k_h.reshape(requests, new_tokens, HEAD_DIM)
        v_h = v_h.reshape(requests, new_tokens, sub_width)
        fresh_scores = (
            jnp.einsum("rtd,rud->rtu", q_h, k_h, preferred_element_type=jnp.float32) * score_scale
        )
        fresh_scores = jnp.where(causal[None], fresh_scores, very_negative)
        fresh_max = jnp.max(fresh_scores, axis=2)
        fresh_weights = jnp.where(causal[None], jnp.exp(fresh_scores - fresh_max[..., None]), 0.0)
        fresh_sum = jnp.sum(fresh_weights, axis=2)
        fresh_out = jnp.einsum(
            "rtu,rud->rtd",
            fresh_weights.astype(jnp.bfloat16),
            v_h,
            preferred_element_type=jnp.float32,
        )
        fresh_max = fresh_max.reshape(rows)
        fresh_sum = fresh_sum.reshape(rows)
        fresh_out = fresh_out.reshape(rows, sub_width)

        top = jnp.maximum(jnp.max(got_max, axis=0), fresh_max)
        scale_cache = jnp.exp(got_max - top[None, :])
        scale_fresh = jnp.exp(fresh_max - top)
        denom = jnp.sum(got_sum * scale_cache, axis=0) + fresh_sum * scale_fresh
        numer = jnp.sum(got_out * scale_cache[:, None, :], axis=0).T + fresh_out * scale_fresh[:, None]
        my_cols = (numer / denom[:, None]).astype(jnp.bfloat16)

        update = jnp.dot(my_cols, w_out[layer_index], preferred_element_type=jnp.float32)
        update = update + jnp.dot(activated, w_fc2[layer_index], preferred_element_type=jnp.float32)
        update = allreduce_chip(update.reshape(2, all_count // 2, -1, 128), tp_count, jnp.bfloat16)
        hidden_state = hidden_state + update.reshape(rows, width).astype(jnp.float32)
    return hidden_state.reshape(requests, new_tokens, width)


def solution(mesh):
    in_specs = (
        P(),
        P(("seq", "tp"), None),
        P(),
        P(),
        P(),
        P("seq", None),
        P(None, "seq", "tp"),
        P(None, "seq", "tp"),
        P(),
        P(),
        P(None, "seq", None, "tp"),
        P(None, "seq", "tp"),
        P(None, "tp"),
        P(None, ("tp", "seq"), None),
        P(None, ("tp", "seq"), None),
    )
    out_specs = P()
    return jax.shard_map(
        per_device, mesh=mesh, in_specs=in_specs, out_specs=out_specs, check_vma=False
    )
```

profile of v0, /device:TPU:25, one launch (start us, length us, event | category | flops | bytes accessed | tf_op | source)
XLA Modules:
  0.0 317.8 jit_solution(17675585683017830382)
XLA Ops:
  4.2 2.4 select_select_fusion.x_ref
  11.3 64.3 %shard_map.145 = (bf16[2,64,32,128]{3,2,1,0:T(8,128)(2,1)}, bf16[32,176,128]{2,1,0:T(8,128)(2,1)}) custom-call(bf16[2,64,32,128]{3,2,1,0:T(8,128)(2,1)} %select_select_fusion.x_ref, bf16[32,176,128]{2,1,0:T(8,128)(2,1)} %pad_maximum_fusion.w_ref), custom_call_target="tpu_custom_call" | custom-call | tf_op jit(solution)/shard_map/pallas_call | solution.py:300
  75.6 1.9 convert_reduce_fusion
  79.9 2.1 fusion.5
  83.5 3.8 %copy.193 = bf16[32,176,128]{1,2,0:T(8,128)(2,1)} copy(bf16[32,176,128]{2,1,0:T(8,128)(2,1)} %get-tuple-element.14) | data formatting | bytes 2883584 | tf_op jit(solution)/shard_map/pallas_call | solution.py:300
  87.3 2.7 fusion.113
  91.9 11.8 %shard_map.146 = bf16[32,16,256]{2,1,0:T(8,128)(2,1)} custom-call(bf16[32,16,256]{2,1,0:T(8,128)(2,1)} %broadcast_in_dim.272.x_ref), custom_call_target="tpu_custom_call" | custom-call | tf_op jit(solution)/shard_map/pallas_call | solution.py:353
  106.7 1.9 broadcast_in_dim.280
  108.6 3.0 convert_element_type.96.mask_ref
  111.6 14.2 %shard_map.147 = (f32[8,256,128]{2,1,0:T(8,128)}, f32[8,256,128]{2,1,0:T(8,128)}, f32[8,256,128]{2,1,0:T(8,128)}) custom-call(bf16[8,256,128]{2,1,0:T(8,128)(2,1)} %broadcast_select_fusion.1.q_ref, bf16[2,2048,512]{2,1,0:T(8,128)(2,1)} %k_ref.3, bf16[2,2048,512]{2,1,0:T(8,128)(2,1)} %v_ref.3, f32[256,2048]{1,0:T(8,128)} %convert_element_type.96.mask_ref), custom_call_target="tpu_custom_call" | custom-call | tf_op jit(solution)/shard_map/pallas_call | solution.py:389
  125.8 2.1 slice_reduce_fusion.2
  130.9 19.0 %shard_map.148 = f32[32,24,256]{2,1,0:T(8,128)} custom-call(f32[32,24,256]{2,1,0:T(8,128)} %maximum_maximum_fusion.x_ref), custom_call_target="tpu_custom_call" | custom-call | tf_op jit(solution)/shard_map/pallas_call | solution.py:353
  157.4 3.5 %convolution_add_fusion.1 = f32[256,2048]{1,0:T(8,128)} fusion(f32[256,2048]{1,0:T(8,128)} %fusion.29, bf16[2,64,2048]{2,1,0:T(8,128)(2,1)S(1)} %copy-done.5, f32[256,176]{0,1:T(8,128)S(1)} %fusion.120, f32[64]{0:T(128)S(1)} %get-tuple-element.60), kind=kOutput, calls=%fused_computation.5 | convolution fusion | flops 67796992 | bytes 4522496 | tf_op jit(solution)/shard_map/dot_general | solution.py:610
  160.8 2.7 reshape.521.x_ref
  163.5 35.8 %shard_map.149 = bf16[2,64,32,128]{3,2,1,0:T(8,128)(2,1)} custom-call(f32[2,64,32,128]{3,2,1,0:T(8,128)} %reshape.521.x_ref), custom_call_target="tpu_custom_call" | custom-call | tf_op jit(solution)/shard_map/pallas_call | solution.py:243
  199.4 1.9 fusion.6
  203.7 2.1 add_convert_fusion
  210.0 12.0 %shard_map.150 = bf16[32,16,256]{2,1,0:T(8,128)(2,1)} custom-call(bf16[32,16,256]{2,1,0:T(8,128)(2,1)} %broadcast_in_dim.288.x_ref), custom_call_target="tpu_custom_call" | custom-call | tf_op jit(solution)/shard_map/pallas_call | solution.py:353
  224.1 14.2 %shard_map.151 = (f32[8,256,128]{2,1,0:T(8,128)}, f32[8,256,128]{2,1,0:T(8,128)}, f32[8,256,128]{2,1,0:T(8,128)}) custom-call(bf16[8,256,128]{2,1,0:T(8,128)(2,1)} %broadcast_select_fusion.q_ref, bf16[2,2048,512]{2,1,0:T(8,128)(2,1)} %k_ref.3, bf16[2,2048,512]{2,1,0:T(8,128)(2,1)} %v_ref.3, f32[256,2048]{1,0:T(8,128)} %convert_element_type.96.mask_ref), custom_call_target="tpu_custom_call" | custom-call | tf_op jit(solution)/shard_map/pallas_call | solution.py:389
  244.3 19.9 %shard_map.152 = f32[32,24,256]{2,1,0:T(8,128)} custom-call(f32[32,24,256]{2,1,0:T(8,128)} %maximum_maximum_fusion.1.x_ref), custom_call_target="tpu_custom_call" | custom-call | tf_op jit(solution)/shard_map/pallas_call | solution.py:353
  271.5 2.7 reshape.531.x_ref
  274.3 37.2 %shard_map.153 = bf16[2,64,32,128]{3,2,1,0:T(8,128)(2,1)} custom-call(f32[2,64,32,128]{3,2,1,0:T(8,128)} %reshape.531.x_ref), custom_call_target="tpu_custom_call" | custom-call | tf_op jit(solution)/shard_map/pallas_call | solution.py:243
  311.5 3.4 %convert_add_fusion.1 = f32[2,64,32,128]{3,2,1,0:T(8,128)} fusion(bf16[2,64,32,128]{3,2,1,0:T(8,128)(2,1)} %shard_map.153, bf16[2,64,32,128]{3,2,1,0:T(8,128)(2,1)} %shard_map.149, bf16[2,64,32,128]{3,2,1,0:T(8,128)(2,1)S(1)} %copy-done.2), kind=kLoop, calls=%fused_computation.12 | loop fusion | flops 2621440 | bytes 5242880 | tf_op jit(solution)/shard_map/add | solution.py:612
  314.9 2.9 add.280
  (224 shorter events, 49.2 us)
Async XLA Ops:
  0.0 1.4 copy-start
  2.8 0.9 copy-start.13
  2.8 3.8 %copy-start.4 = (bf16[2,64,2048]{2,1,0:T(8,128)(2,1)S(1)}, bf16[2,64,2048]{2,1,0:T(8,128)(2,1)}, u32[]{:S(2)}) copy-start(bf16[2,64,2048]{2,1,0:T(8,128)(2,1)} %param.26) | copy-start | bytes 1572868
  6.6 2.2 copy-start.6
  10.0 65.5 %copy-start.8 = (f32[2,2048]{1,0:T(2,128)S(1)}, f32[2,2048]{1,0:T(2,128)}, u32[]{:S(2)}) copy-start(f32[2,2048]{1,0:T(2,128)} %param.24) | copy-start | bytes 49156
  10.0 65.5 %copy-start.9 = (f32[2,2048]{1,0:T(2,128)S(1)}, f32[2,2048]{1,0:T(2,128)}, u32[]{:S(2)}) copy-start(f32[2,2048]{1,0:T(2,128)} %param.23) | copy-start | bytes 49156
  75.5 2.6 copy-start.2
  90.0 0.7 copy-start.23
  90.0 0.8 copy-start.24
  90.6 15.5 %copy-start.21 = (s32[16,2]{0,1:T(2,128)S(1)}, s32[16,2]{0,1:T(2,128)}, u32[]{:S(2)}) copy-start(s32[16,2]{0,1:T(2,128)} %param.20) | copy-start | bytes 388
  90.7 61.2 %copy-start.11 = (f32[16]{0:T(128)}, f32[16]{0:T(128)S(1)}, u32[]{:S(2)}) copy-start(f32[16]{0:T(128)S(1)} %multiply_exponential_fusion) | copy-start | bytes 196
  105.0 24.6 %copy-start.16 = (pred[2,2]{1,0:T(4,128)(4,1)}, pred[2,2]{1,0:T(4,128)(4,1)S(1)}, u32[]{:S(2)}) copy-start(pred[2,2]{1,0:T(4,128)(4,1)S(1)} %iota_compare_fusion.3) | copy-start | bytes 16
  129.9 22.2 %copy-start.18 = (f32[24]{0:T(128)}, f32[24]{0:T(128)S(1)}, u32[]{:S(2)}) copy-start(f32[24]{0:T(128)S(1)} %pad.15.clone) | copy-start | bytes 292
  130.9 24.1 %copy-start.7 = (bf16[2,16,2048]{2,1,0:T(8,128)(2,1)S(1)}, bf16[2,16,2048]{2,1,0:T(8,128)(2,1)}, u32[]{:S(2)}) copy-start(bf16[2,16,2048]{2,1,0:T(8,128)(2,1)} %param.28) | copy-start | bytes 393220
  152.1 4.6 %copy-start.10 = (f32[2,2048]{1,0:T(2,128)S(1)}, f32[2,2048]{1,0:T(2,128)}, u32[]{:S(2)}) copy-start(f32[2,2048]{1,0:T(2,128)} %param.27) | copy-start | bytes 49156
  152.1 5.3 %copy-start.5 = (bf16[2,64,2048]{2,1,0:T(8,128)(2,1)S(1)}, bf16[2,64,2048]{2,1,0:T(8,128)(2,1)}, u32[]{:S(2)}) copy-start(bf16[2,64,2048]{2,1,0:T(8,128)(2,1)} %param.29) | copy-start | bytes 1572868
  152.6 1.8 copy-start.14
  199.3 2.5 copy-start.3
  205.7 3.3 %copy-start.12 = (f32[16]{0:T(128)S(1)}, f32[16]{0:T(128)}, u32[]{:S(2)}) copy-start(f32[16]{0:T(128)} %copy-done.11) | copy-start | bytes 196
  238.3 4.8 %copy-start.17 = (pred[2,2]{1,0:T(4,128)(4,1)S(1)}, pred[2,2]{1,0:T(4,128)(4,1)}, u32[]{:S(2)}) copy-start(pred[2,2]{1,0:T(4,128)(4,1)} %copy-done.16) | copy-start | bytes 16
  241.5 1.8 copy-start.19
  243.3 23.5 %copy-start.15 = (pred[4,4]{1,0:T(4,128)(4,1)S(1)}, pred[4,4]{1,0:T(4,128)(4,1)}, u32[]{:S(2)}) copy-start(pred[4,4]{1,0:T(4,128)(4,1)} %copy-done.14) | copy-start | bytes 52
  266.4 3.3 %copy-start.20 = (f32[64]{0:T(128)S(1)}, f32[64]{0:T(128)}, u32[]{:S(2)}) copy-start(f32[64]{0:T(128)} %get-tuple-element.61) | copy-start | bytes 772
  311.5 6.3 %copy-start.1 = (bf16[400,2048]{1,0:T(8,128)(2,1)S(1)}, bf16[400,2048]{1,0:T(8,128)(2,1)}, u32[]{:S(2)}) copy-start(bf16[400,2048]{1,0:T(8,128)(2,1)} %param.16) | copy-start | bytes 4915204
  (1 other events, 0.7 us)
where the time goes:
time: 321 us; the launch traced here: 318 us
  Pallas kernels  228 us (71%)
  local copies, waits for them, and re-layouts  48.4 us (15%)
  other arithmetic  29.2 us (9%)
  matrix products  10.7 us (3%)
    pallas_call x2, Pallas kernels, allreduce_chip(): pl.pallas_call(functools.partial(_allreduce_chip_kernel, tp_count), out_s...  73 us
    pallas_call x1, Pallas kernels, opening(): pl.pallas_call(functools.partial(_opening_kernel, tp_count), out_shape=(j...  64.3 us
    pallas_call x4, Pallas kernels, all_to_all(): pl.pallas_call(functools.partial(_all_to_all_kernel, n, whole, tp_count),...  62.7 us
    pallas_call x2, Pallas kernels, cache_attention(): pl.pallas_call(functools.partial(_attention_kernel, scale), grid=(heads,)...  28.4 us

commit v1 on v0

--- a/solution.py
+++ b/solution.py
@@ -365,6 +365,55 @@
             collective_id=_kernel_id(("all_to_all", whole, x.shape, str(x.dtype))),
         ),
     )(x)
+
+
+def _all_to_all_pair_kernel(n, whole, tp_count, xa_ref, xb_ref, oa_ref, ob_ref, bufa, bufb, sa, ra, sb, rb):
+    me, peer = _group_ids(whole, tp_count)
+    _enter(n, me, peer)
+
+    def start(i, carry):
+        j = lax.rem(me + i, n)
+        _rcopy(xa_ref.at[j], bufa.at[me], sa.at[j], ra.at[me], peer(j)).start()
+        _rcopy(xb_ref.at[j], bufb.at[me], sb.at[j], rb.at[me], peer(j)).start()
+        return carry
+
+    lax.fori_loop(1, n, start, 0)
+
+    def finish(i, carry):
+        j = lax.rem(me + i, n)
+        _rcopy(xa_ref.at[j], bufa.at[j], sa.at[j], ra.at[j], peer(j)).wait_recv()
+        _rcopy(xb_ref.at[j], bufb.at[j], sb.at[j], rb.at[j], peer(j)).wait_recv()
+        _rcopy(xa_ref.at[j], bufa.at[me], sa.at[j], ra.at[me], peer(j)).wait_send()
+        _rcopy(xb_ref.at[j], bufb.at[me], sb.at[j], rb.at[me], peer(j)).wait_send()
+        return carry
+
+    lax.fori_loop(1, n, finish, 0)
+    bufa[me] = xa_ref[me]
+    bufb[me] = xb_ref[me]
+    oa_ref[...] = bufa[...]
+    ob_ref[...] = bufb[...]
+
+
+def all_to_all_pair(xa, xb, whole, tp_count):
+    n = xa.shape[0]
+    return pl.pallas_call(
+        functools.partial(_all_to_all_pair_kernel, n, whole, tp_count),
+        out_shape=(jax.ShapeDtypeStruct(xa.shape, xa.dtype), jax.ShapeDtypeStruct(xb.shape, xb.dtype)),
+        in_specs=[pl.BlockSpec(memory_space=pltpu.VMEM)] * 2,
+        out_specs=(pl.BlockSpec(memory_space=pltpu.VMEM), pl.BlockSpec(memory_space=pltpu.VMEM)),
+        scratch_shapes=[
+            pltpu.VMEM(xa.shape, xa.dtype),
+            pltpu.VMEM(xb.shape, xb.dtype),
+            pltpu.SemaphoreType.DMA((n,)),
+            pltpu.SemaphoreType.DMA((n,)),
+            pltpu.SemaphoreType.DMA((n,)),
+            pltpu.SemaphoreType.DMA((n,)),
+        ],
+        compiler_params=pltpu.CompilerParams(
+            has_side_effects=True,
+            collective_id=_kernel_id(("all_to_all_pair", whole, xa.shape, xb.shape)),
+        ),
+    )(xa, xb)
 
 
 def _attention_kernel(scale, q_ref, k_ref, v_ref, mask_ref, o_ref, m_ref, l_ref):
@@ -572,11 +621,11 @@
         max_rows = jnp.repeat(part_max, pieces, axis=0)[:, None, :]
         sum_rows = jnp.repeat(part_sum, pieces, axis=0)[:, None, :]
         pad_rows = jnp.zeros((heads_local * pieces, 6, rows), jnp.float32)
-        message = jnp.concatenate([out_pieces, max_rows, sum_rows, pad_rows], axis=1)
-        received = all_to_all(message, False, tp_count)
-        got_out = received[:, :sub_width, :]
-        got_max = received[:, sub_width, :]
-        got_sum = received[:, sub_width + 1, :]
+        stats = jnp.concatenate([max_rows, sum_rows, pad_rows], axis=1)
+        got_out, got_stats = all_to_all_pair(out_pieces.astype(jnp.bfloat16), stats, False, tp_count)
+        got_out = got_out.astype(jnp.float32)
+        got_max = got_stats[:, 0, :]
+        got_sum = got_stats[:, 1, :]
 
         q_h = lax.dynamic_index_in_dim(queries, my_head, 1, keepdims=False)
         q_h = q_h.reshape(requests, new_tokens, HEAD_DIM)

time: 321 us -> 316 us (0.984)
  Pallas kernels: 228 us -> 222 us
  local copies, waits for them, and re-layouts: 48.4 us -> 52 us
    pallas_call x4 -> x2, Pallas kernels: 62.7 us -> 23.8 us  [all_to_all(): pl.pallas_call(functools.partial(_all_to_all_kernel, n, whole, tp_count),...]
    pallas_call x0 -> x2, Pallas kernels: none -> 32 us  [all_to_all_pair(): pl.pallas_call(functools.partial(_all_to_all_pair_kernel, n, whole, tp_co...]
where the time goes in v1:
time: 316 us; the launch traced here: 313 us
  Pallas kernels  222 us (70%)
  local copies, waits for them, and re-layouts  52 us (16%)
  other arithmetic  27.9 us (9%)
  matrix products  10.7 us (3%)
    pallas_call x2, Pallas kernels, allreduce_chip(): pl.pallas_call(functools.partial(_allreduce_chip_kernel, tp_count), out_s...  73 us
    pallas_call x1, Pallas kernels, opening(): pl.pallas_call(functools.partial(_opening_kernel, tp_count), out_shape=(j...  64.3 us
    pallas_call x2, Pallas kernels, all_to_all_pair(): pl.pallas_call(functools.partial(_all_to_all_pair_kernel, n, whole, tp_co...  32 us
    pallas_call x2, Pallas kernels, cache_attention(): pl.pallas_call(functools.partial(_attention_kernel, scale), grid=(heads,)...  28.4 us
    pallas_call x2, Pallas kernels, all_to_all(): pl.pallas_call(functools.partial(_all_to_all_kernel, n, whole, tp_count),...  23.8 us

profile of v1, /device:TPU:25, one launch (start us, length us, event | category | flops | bytes accessed | tf_op | source)
XLA Modules:
  0.0 313.1 jit_solution(14126256844848544987)
XLA Ops:
  4.2 2.4 select_select_fusion.x_ref
  11.2 64.3 %shard_map.145 = (bf16[2,64,32,128]{3,2,1,0:T(8,128)(2,1)}, bf16[32,176,128]{2,1,0:T(8,128)(2,1)}) custom-call(bf16[2,64,32,128]{3,2,1,0:T(8,128)(2,1)} %select_select_fusion.x_ref, bf16[32,176,128]{2,1,0:T(8,128)(2,1)} %pad_maximum_fusion.w_ref), custom_call_target="tpu_custom_call" | custom-call | tf_op jit(solution)/shard_map/pallas_call | solution.py:300
  75.5 1.9 convert_reduce_fusion
  79.9 2.1 fusion.5
  83.5 3.8 %copy.193 = bf16[32,176,128]{1,2,0:T(8,128)(2,1)} copy(bf16[32,176,128]{2,1,0:T(8,128)(2,1)} %get-tuple-element.18) | data formatting | bytes 2883584 | tf_op jit(solution)/shard_map/pallas_call | solution.py:300
  87.3 2.7 fusion.113
  92.3 11.8 %shard_map.146 = bf16[32,16,256]{2,1,0:T(8,128)(2,1)} custom-call(bf16[32,16,256]{2,1,0:T(8,128)(2,1)} %broadcast_in_dim.272.x_ref), custom_call_target="tpu_custom_call" | custom-call | tf_op jit(solution)/shard_map/pallas_call | solution.py:353
  108.5 1.9 broadcast_in_dim.280
  110.5 3.0 convert_element_type.120.mask_ref
  113.4 14.2 %shard_map.147 = (f32[8,256,128]{2,1,0:T(8,128)}, f32[8,256,128]{2,1,0:T(8,128)}, f32[8,256,128]{2,1,0:T(8,128)}) custom-call(bf16[8,256,128]{2,1,0:T(8,128)(2,1)} %broadcast_select_fusion.1.q_ref, bf16[2,2048,512]{2,1,0:T(8,128)(2,1)} %k_ref.3, bf16[2,2048,512]{2,1,0:T(8,128)(2,1)} %v_ref.3, f32[256,2048]{1,0:T(8,128)} %convert_element_type.120.mask_ref), custom_call_target="tpu_custom_call" | custom-call | tf_op jit(solution)/shard_map/pallas_call | solution.py:438
  127.6 2.1 slice_reduce_fusion.2
  133.3 15.7 %shard_map.148 = (bf16[32,16,256]{2,1,0:T(8,128)(2,1)}, f32[32,8,256]{2,1,0:T(8,128)}) custom-call(bf16[32,16,256]{2,1,0:T(8,128)(2,1)} %bitcast.173, f32[32,8,256]{2,1,0:T(8,128)} %maximum_maximum_fusion.xb_ref), custom_call_target="tpu_custom_call" | custom-call | tf_op jit(solution)/shard_map/pallas_call | solution.py:399
  154.9 3.5 %convolution_add_fusion.1 = f32[256,2048]{1,0:T(8,128)} fusion(f32[256,2048]{1,0:T(8,128)} %fusion.29, bf16[2,64,2048]{2,1,0:T(8,128)(2,1)S(1)} %copy-done.5, f32[256,176]{0,1:T(8,128)S(1)} %fusion.118, f32[64]{0:T(128)S(1)} %get-tuple-element.62), kind=kOutput, calls=%fused_computation.5 | convolution fusion | flops 67796992 | bytes 4522496 | tf_op jit(solution)/shard_map/dot_general | solution.py:659
  158.4 2.7 reshape.520.x_ref
  161.0 36.1 %shard_map.149 = bf16[2,64,32,128]{3,2,1,0:T(8,128)(2,1)} custom-call(f32[2,64,32,128]{3,2,1,0:T(8,128)} %reshape.520.x_ref), custom_call_target="tpu_custom_call" | custom-call | tf_op jit(solution)/shard_map/pallas_call | solution.py:243
  197.1 1.9 fusion.6
  201.5 2.1 add_convert_fusion
  208.1 12.0 %shard_map.150 = bf16[32,16,256]{2,1,0:T(8,128)(2,1)} custom-call(bf16[32,16,256]{2,1,0:T(8,128)(2,1)} %broadcast_in_dim.288.x_ref), custom_call_target="tpu_custom_call" | custom-call | tf_op jit(solution)/shard_map/pallas_call | solution.py:353
  223.7 14.2 %shard_map.151 = (f32[8,256,128]{2,1,0:T(8,128)}, f32[8,256,128]{2,1,0:T(8,128)}, f32[8,256,128]{2,1,0:T(8,128)}) custom-call(bf16[8,256,128]{2,1,0:T(8,128)(2,1)} %broadcast_select_fusion.q_ref, bf16[2,2048,512]{2,1,0:T(8,128)(2,1)} %k_ref.3, bf16[2,2048,512]{2,1,0:T(8,128)(2,1)} %v_ref.3, f32[256,2048]{1,0:T(8,128)} %convert_element_type.120.mask_ref), custom_call_target="tpu_custom_call" | custom-call | tf_op jit(solution)/shard_map/pallas_call | solution.py:438
  244.4 16.4 %shard_map.152 = (bf16[32,16,256]{2,1,0:T(8,128)(2,1)}, f32[32,8,256]{2,1,0:T(8,128)}) custom-call(bf16[32,16,256]{2,1,0:T(8,128)(2,1)} %bitcast.172, f32[32,8,256]{2,1,0:T(8,128)} %maximum_maximum_fusion.1.xb_ref), custom_call_target="tpu_custom_call" | custom-call | tf_op jit(solution)/shard_map/pallas_call | solution.py:399
  267.1 2.7 reshape.529.x_ref
  269.9 36.9 %shard_map.153 = bf16[2,64,32,128]{3,2,1,0:T(8,128)(2,1)} custom-call(f32[2,64,32,128]{3,2,1,0:T(8,128)} %reshape.529.x_ref), custom_call_target="tpu_custom_call" | custom-call | tf_op jit(solution)/shard_map/pallas_call | solution.py:243
  306.8 3.4 %convert_add_fusion.1 = f32[2,64,32,128]{3,2,1,0:T(8,128)} fusion(bf16[2,64,32,128]{3,2,1,0:T(8,128)(2,1)} %shard_map.153, bf16[2,64,32,128]{3,2,1,0:T(8,128)(2,1)} %shard_map.149, bf16[2,64,32,128]{3,2,1,0:T(8,128)(2,1)S(1)} %copy-done.2), kind=kLoop, calls=%fused_computation.12 | loop fusion | flops 2621440 | bytes 5242880 | tf_op jit(solution)/shard_map/add | solution.py:661
  310.2 2.9 add.280
  (210 shorter events, 51.4 us)
Async XLA Ops:
  0.0 1.4 copy-start
  2.8 0.9 copy-start.11
  2.8 3.8 %copy-start.6 = (bf16[2,64,3,512]{3,1,2,0:T(8,128)(2,1)S(1)}, bf16[2,64,3,512]{3,1,2,0:T(8,128)(2,1)}, u32[]{:S(2)}) copy-start(bf16[2,64,3,512]{3,1,2,0:T(8,128)(2,1)} %param.25) | copy-start | bytes 1179652
  6.6 1.2 copy-start.4
  75.5 2.5 copy-start.2
  75.5 4.3 %copy-start.8 = (f32[2,2048]{1,0:T(2,128)S(1)}, f32[2,2048]{1,0:T(2,128)}, u32[]{:S(2)}) copy-start(f32[2,2048]{1,0:T(2,128)} %param.23) | copy-start | bytes 49156
  75.5 4.4 %copy-start.9 = (f32[2,2048]{1,0:T(2,128)S(1)}, f32[2,2048]{1,0:T(2,128)}, u32[]{:S(2)}) copy-start(f32[2,2048]{1,0:T(2,128)} %param.24) | copy-start | bytes 49156
  90.0 0.7 copy-start.13
  90.0 0.7 copy-start.14
  90.0 0.8 copy-start.15
  92.3 15.7 %copy-start.12 = (s32[16,2]{0,1:T(2,128)S(1)}, s32[16,2]{0,1:T(2,128)}, u32[]{:S(2)}) copy-start(s32[16,2]{0,1:T(2,128)} %param.20) | copy-start | bytes 388
  132.4 20.6 %copy-start.7 = (bf16[2,16,2048]{2,1,0:T(8,128)(2,1)S(1)}, bf16[2,16,2048]{2,1,0:T(8,128)(2,1)}, u32[]{:S(2)}) copy-start(bf16[2,16,2048]{2,1,0:T(8,128)(2,1)} %param.28) | copy-start | bytes 393220
  148.9 5.9 %copy-start.10 = (f32[2,2048]{1,0:T(2,128)S(1)}, f32[2,2048]{1,0:T(2,128)}, u32[]{:S(2)}) copy-start(f32[2,2048]{1,0:T(2,128)} %param.27) | copy-start | bytes 49156
  148.9 6.0 %copy-start.5 = (bf16[2,64,2048]{2,1,0:T(8,128)(2,1)S(1)}, bf16[2,64,2048]{2,1,0:T(8,128)(2,1)}, u32[]{:S(2)}) copy-start(bf16[2,64,2048]{2,1,0:T(8,128)(2,1)} %param.29) | copy-start | bytes 1572868
  197.1 2.5 copy-start.3
  306.8 6.3 %copy-start.1 = (bf16[400,2048]{1,0:T(8,128)(2,1)S(1)}, bf16[400,2048]{1,0:T(8,128)(2,1)}, u32[]{:S(2)}) copy-start(bf16[400,2048]{1,0:T(8,128)(2,1)} %param.16) | copy-start | bytes 4915204

commit v2 on v1

--- a/solution.py
+++ b/solution.py
@@ -657,7 +657,9 @@
 
         update = jnp.dot(my_cols, w_out[layer_index], preferred_element_type=jnp.float32)
         update = update + jnp.dot(activated, w_fc2[layer_index], preferred_element_type=jnp.float32)
-        update = allreduce_chip(update.reshape(2, all_count // 2, -1, 128), tp_count, jnp.bfloat16)
+        update = allreduce_chip(
+            update.astype(jnp.bfloat16).reshape(2, all_count // 2, -1, 128), tp_count
+        )
         hidden_state = hidden_state + update.reshape(rows, width).astype(jnp.float32)
     return hidden_state.reshape(requests, new_tokens, width)
 

time: 316 us -> 308 us (0.975)
  no operation moved by 1% of the time
where the time goes in v2:
time: 308 us; the launch traced here: 305 us
  Pallas kernels  219 us (71%)
  local copies, waits for them, and re-layouts  49.2 us (16%)
  other arithmetic  27.9 us (9%)
  matrix products  8.05 us (3%)
    pallas_call x2, Pallas kernels, allreduce_chip(): pl.pallas_call(functools.partial(_allreduce_chip_kernel, tp_count), out_s...  70.9 us
    pallas_call x1, Pallas kernels, opening(): pl.pallas_call(functools.partial(_opening_kernel, tp_count), out_shape=(j...  64.3 us
    pallas_call x2, Pallas kernels, all_to_all_pair(): pl.pallas_call(functools.partial(_all_to_all_pair_kernel, n, whole, tp_co...  31.8 us
    pallas_call x2, Pallas kernels, cache_attention(): pl.pallas_call(functools.partial(_attention_kernel, scale), grid=(heads,)...  28.4 us
    pallas_call x2, Pallas kernels, all_to_all(): pl.pallas_call(functools.partial(_all_to_all_kernel, n, whole, tp_count),...  23.8 us

profile of v2, /device:TPU:25, one launch (start us, length us, event | category | flops | bytes accessed | tf_op | source)
XLA Modules:
  0.0 305.3 jit_solution(12030626331839761997)
XLA Ops:
  4.2 2.4 select_select_fusion.x_ref
  11.2 64.3 %shard_map.145 = (bf16[2,64,32,128]{3,2,1,0:T(8,128)(2,1)}, bf16[32,176,128]{2,1,0:T(8,128)(2,1)}) custom-call(bf16[2,64,32,128]{3,2,1,0:T(8,128)(2,1)} %select_select_fusion.x_ref, bf16[32,176,128]{2,1,0:T(8,128)(2,1)} %pad_maximum_fusion.w_ref), custom_call_target="tpu_custom_call" | custom-call | tf_op jit(solution)/shard_map/pallas_call | solution.py:300
  75.5 1.9 convert_reduce_fusion
  79.9 2.1 fusion.7
  83.5 3.8 %copy.193 = bf16[32,176,128]{1,2,0:T(8,128)(2,1)} copy(bf16[32,176,128]{2,1,0:T(8,128)(2,1)} %get-tuple-element.18) | data formatting | bytes 2883584 | tf_op jit(solution)/shard_map/pallas_call | solution.py:300
  87.3 2.7 fusion.115
  92.2 11.8 %shard_map.146 = bf16[32,16,256]{2,1,0:T(8,128)(2,1)} custom-call(bf16[32,16,256]{2,1,0:T(8,128)(2,1)} %broadcast_in_dim.272.x_ref), custom_call_target="tpu_custom_call" | custom-call | tf_op jit(solution)/shard_map/pallas_call | solution.py:353
  108.5 1.9 broadcast_in_dim.280
  110.4 3.0 convert_element_type.126.mask_ref
  113.4 14.2 %shard_map.147 = (f32[8,256,128]{2,1,0:T(8,128)}, f32[8,256,128]{2,1,0:T(8,128)}, f32[8,256,128]{2,1,0:T(8,128)}) custom-call(bf16[8,256,128]{2,1,0:T(8,128)(2,1)} %broadcast_select_fusion.1.q_ref, bf16[2,2048,512]{2,1,0:T(8,128)(2,1)} %k_ref.3, bf16[2,2048,512]{2,1,0:T(8,128)(2,1)} %v_ref.3, f32[256,2048]{1,0:T(8,128)} %convert_element_type.126.mask_ref), custom_call_target="tpu_custom_call" | custom-call | tf_op jit(solution)/shard_map/pallas_call | solution.py:438
  127.6 2.1 slice_reduce_fusion.2
  133.2 15.6 %shard_map.148 = (bf16[32,16,256]{2,1,0:T(8,128)(2,1)}, f32[32,8,256]{2,1,0:T(8,128)}) custom-call(bf16[32,16,256]{2,1,0:T(8,128)(2,1)} %bitcast.173, f32[32,8,256]{2,1,0:T(8,128)} %maximum_maximum_fusion.xb_ref), custom_call_target="tpu_custom_call" | custom-call | tf_op jit(solution)/shard_map/pallas_call | solution.py:399
  153.0 1.8 fusion.31
  154.9 2.1 fusion
  158.3 35.0 %shard_map.149 = bf16[2,64,32,128]{3,2,1,0:T(8,128)(2,1)} custom-call(bf16[2,64,32,128]{3,2,1,0:T(8,128)(2,1)} %reshape.520.x_ref), custom_call_target="tpu_custom_call" | custom-call | tf_op jit(solution)/shard_map/pallas_call | solution.py:243
  193.3 1.9 fusion.8
  197.7 2.1 add_convert_fusion
  201.3 1.8 fusion.123
  204.3 12.0 %shard_map.150 = bf16[32,16,256]{2,1,0:T(8,128)(2,1)} custom-call(bf16[32,16,256]{2,1,0:T(8,128)(2,1)} %broadcast_in_dim.288.x_ref), custom_call_target="tpu_custom_call" | custom-call | tf_op jit(solution)/shard_map/pallas_call | solution.py:353
  219.9 14.2 %shard_map.151 = (f32[8,256,128]{2,1,0:T(8,128)}, f32[8,256,128]{2,1,0:T(8,128)}, f32[8,256,128]{2,1,0:T(8,128)}) custom-call(bf16[8,256,128]{2,1,0:T(8,128)(2,1)} %broadcast_select_fusion.q_ref, bf16[2,2048,512]{2,1,0:T(8,128)(2,1)} %k_ref.3, bf16[2,2048,512]{2,1,0:T(8,128)(2,1)} %v_ref.3, f32[256,2048]{1,0:T(8,128)} %convert_element_type.126.mask_ref), custom_call_target="tpu_custom_call" | custom-call | tf_op jit(solution)/shard_map/pallas_call | solution.py:438
  240.6 16.1 %shard_map.152 = (bf16[32,16,256]{2,1,0:T(8,128)(2,1)}, f32[32,8,256]{2,1,0:T(8,128)}) custom-call(bf16[32,16,256]{2,1,0:T(8,128)(2,1)} %bitcast.172, f32[32,8,256]{2,1,0:T(8,128)} %maximum_maximum_fusion.1.xb_ref), custom_call_target="tpu_custom_call" | custom-call | tf_op jit(solution)/shard_map/pallas_call | solution.py:399
  263.1 35.9 %shard_map.153 = bf16[2,64,32,128]{3,2,1,0:T(8,128)(2,1)} custom-call(bf16[2,64,32,128]{3,2,1,0:T(8,128)(2,1)} %reshape.529.x_ref), custom_call_target="tpu_custom_call" | custom-call | tf_op jit(solution)/shard_map/pallas_call | solution.py:243
  299.0 3.4 %convert_add_fusion.1 = f32[2,64,32,128]{3,2,1,0:T(8,128)} fusion(bf16[2,64,32,128]{3,2,1,0:T(8,128)(2,1)} %shard_map.153, bf16[2,64,32,128]{3,2,1,0:T(8,128)(2,1)} %shard_map.149, bf16[2,64,32,128]{3,2,1,0:T(8,128)(2,1)S(1)} %copy-done.2), kind=kLoop, calls=%fused_computation.14 | loop fusion | flops 2621440 | bytes 5242880 | tf_op jit(solution)/shard_map/add | solution.py:663
  302.4 2.9 add.280
  (210 shorter events, 49.1 us)
Async XLA Ops:
  0.0 1.4 copy-start
  2.8 0.9 copy-start.11
  2.8 3.8 %copy-start.6 = (bf16[2,64,3,512]{3,1,2,0:T(8,128)(2,1)S(1)}, bf16[2,64,3,512]{3,1,2,0:T(8,128)(2,1)}, u32[]{:S(2)}) copy-start(bf16[2,64,3,512]{3,1,2,0:T(8,128)(2,1)} %param.25) | copy-start | bytes 1179652
  6.6 1.2 copy-start.4
  75.5 2.5 copy-start.2
  75.5 4.3 %copy-start.8 = (f32[2,2048]{1,0:T(2,128)S(1)}, f32[2,2048]{1,0:T(2,128)}, u32[]{:S(2)}) copy-start(f32[2,2048]{1,0:T(2,128)} %param.23) | copy-start | bytes 49156
  75.5 4.4 %copy-start.9 = (f32[2,2048]{1,0:T(2,128)S(1)}, f32[2,2048]{1,0:T(2,128)}, u32[]{:S(2)}) copy-start(f32[2,2048]{1,0:T(2,128)} %param.24) | copy-start | bytes 49156
  90.0 0.7 copy-start.13
  90.0 0.7 copy-start.14
  90.0 0.8 copy-start.15
  92.2 15.7 %copy-start.12 = (s32[16,2]{0,1:T(2,128)S(1)}, s32[16,2]{0,1:T(2,128)}, u32[]{:S(2)}) copy-start(s32[16,2]{0,1:T(2,128)} %param.20) | copy-start | bytes 388
  132.4 20.6 %copy-start.7 = (bf16[2,16,2048]{2,1,0:T(8,128)(2,1)S(1)}, bf16[2,16,2048]{2,1,0:T(8,128)(2,1)}, u32[]{:S(2)}) copy-start(bf16[2,16,2048]{2,1,0:T(8,128)(2,1)} %param.28) | copy-start | bytes 393220
  148.9 5.9 %copy-start.10 = (f32[2,2048]{1,0:T(2,128)S(1)}, f32[2,2048]{1,0:T(2,128)}, u32[]{:S(2)}) copy-start(f32[2,2048]{1,0:T(2,128)} %param.27) | copy-start | bytes 49156
  148.9 6.0 %copy-start.5 = (bf16[2,64,2048]{2,1,0:T(8,128)(2,1)S(1)}, bf16[2,64,2048]{2,1,0:T(8,128)(2,1)}, u32[]{:S(2)}) copy-start(bf16[2,64,2048]{2,1,0:T(8,128)(2,1)} %param.29) | copy-start | bytes 1572868
  193.3 2.5 copy-start.3
  298.9 6.3 %copy-start.1 = (bf16[400,2048]{1,0:T(8,128)(2,1)S(1)}, bf16[400,2048]{1,0:T(8,128)(2,1)}, u32[]{:S(2)}) copy-start(bf16[400,2048]{1,0:T(8,128)(2,1)} %param.16) | copy-start | bytes 4915204

commit v3 on v2

--- a/solution.py
+++ b/solution.py
@@ -418,32 +418,35 @@
 
 def _attention_kernel(scale, q_ref, k_ref, v_ref, mask_ref, o_ref, m_ref, l_ref):
     valid = mask_ref[...] > 0.5
-    scores = lax.dot_general(
-        q_ref[0], k_ref[...], (((1,), (1,)), ((), ())), preferred_element_type=jnp.float32
-    )
-    scores = jnp.where(valid, scores * scale, very_negative)
-    top = jnp.max(scores, axis=1, keepdims=True)
-    weights = jnp.where(valid, jnp.exp(scores - top), 0.0)
-    total = jnp.sum(weights, axis=1, keepdims=True)
-    o_ref[0] = jnp.dot(weights.astype(jnp.bfloat16), v_ref[...], preferred_element_type=jnp.float32)
-    m_ref[0] = jnp.broadcast_to(top, m_ref.shape[1:])
-    l_ref[0] = jnp.broadcast_to(total, l_ref.shape[1:])
+    for half in range(q_ref.shape[0]):
+        scores = lax.dot_general(
+            q_ref[half], k_ref[...], (((1,), (1,)), ((), ())), preferred_element_type=jnp.float32
+        )
+        scores = jnp.where(valid, scores * scale, very_negative)
+        top = jnp.max(scores, axis=1, keepdims=True)
+        weights = jnp.where(valid, jnp.exp(scores - top), 0.0)
+        total = jnp.sum(weights, axis=1, keepdims=True)
+        o_ref[half] = jnp.dot(
+            weights.astype(jnp.bfloat16), v_ref[...], preferred_element_type=jnp.float32
+        )
+        m_ref[half] = jnp.broadcast_to(top, m_ref.shape[1:])
+        l_ref[half] = jnp.broadcast_to(total, l_ref.shape[1:])
 
 
 def cache_attention(q_pad, k_cache, v_cache, mask, layer_index, scale):
     heads, rows, lanes = q_pad.shape
     slots = k_cache.shape[1]
     per_block = lanes // HEAD_DIM
-    out_spec = pl.BlockSpec((1, rows, lanes), lambda h: (h, 0, 0))
+    out_spec = pl.BlockSpec((per_block, rows, lanes), lambda b: (b, 0, 0))
     return pl.pallas_call(
         functools.partial(_attention_kernel, scale),
-        grid=(heads,),
+        grid=(heads // per_block,),
         out_shape=[jax.ShapeDtypeStruct((heads, rows, lanes), jnp.float32)] * 3,
         in_specs=[
-            pl.BlockSpec((1, rows, lanes), lambda h: (h, 0, 0)),
-            pl.BlockSpec((None, slots, lanes), lambda h: (layer_index, 0, h // per_block)),
-            pl.BlockSpec((None, slots, lanes), lambda h: (layer_index, 0, h // per_block)),
-            pl.BlockSpec((rows, slots), lambda h: (0, 0)),
+            pl.BlockSpec((per_block, rows, lanes), lambda b: (b, 0, 0)),
+            pl.BlockSpec((None, slots, lanes), lambda b: (layer_index, 0, b)),
+            pl.BlockSpec((None, slots, lanes), lambda b: (layer_index, 0, b)),
+            pl.BlockSpec((rows, slots), lambda b: (0, 0)),
         ],
         out_specs=[out_spec] * 3,
     )(q_pad, k_cache, v_cache, mask)

time: 308 us -> 305 us (level)
  no operation moved by 1% of the time
where the time goes in v3:
time: 305 us; the launch traced here: 303 us
  Pallas kernels  217 us (71%)
  local copies, waits for them, and re-layouts  49.2 us (16%)
  other arithmetic  27.9 us (9%)
  matrix products  8.04 us (3%)
    pallas_call x2, Pallas kernels, allreduce_chip(): pl.pallas_call(functools.partial(_allreduce_chip_kernel, tp_count), out_s...  70.8 us
    pallas_call x1, Pallas kernels, opening(): pl.pallas_call(functools.partial(_opening_kernel, tp_count), out_shape=(j...  64.3 us
    pallas_call x2, Pallas kernels, all_to_all_pair(): pl.pallas_call(functools.partial(_all_to_all_pair_kernel, n, whole, tp_co...  31.8 us
    pallas_call x2, Pallas kernels, cache_attention(): pl.pallas_call(functools.partial(_attention_kernel, scale), grid=(heads /...  25.9 us
    pallas_call x2, Pallas kernels, all_to_all(): pl.pallas_call(functools.partial(_all_to_all_kernel, n, whole, tp_count),...  23.8 us

profile of v3, /device:TPU:25, one launch (start us, length us, event | category | flops | bytes accessed | tf_op | source)
XLA Modules:
  0.0 302.7 jit_solution(16168756199724861298)
XLA Ops:
  4.2 2.4 select_select_fusion.x_ref
  11.2 64.3 %shard_map.145 = (bf16[2,64,32,128]{3,2,1,0:T(8,128)(2,1)}, bf16[32,176,128]{2,1,0:T(8,128)(2,1)}) custom-call(bf16[2,64,32,128]{3,2,1,0:T(8,128)(2,1)} %select_select_fusion.x_ref, bf16[32,176,128]{2,1,0:T(8,128)(2,1)} %pad_maximum_fusion.w_ref), custom_call_target="tpu_custom_call" | custom-call | tf_op jit(solution)/shard_map/pallas_call | solution.py:300
  75.5 1.9 convert_reduce_fusion
  79.9 2.1 fusion.7
  83.5 3.8 %copy.193 = bf16[32,176,128]{1,2,0:T(8,128)(2,1)} copy(bf16[32,176,128]{2,1,0:T(8,128)(2,1)} %get-tuple-element.18) | data formatting | bytes 2883584 | tf_op jit(solution)/shard_map/pallas_call | solution.py:300
  87.3 2.7 fusion.115
  92.2 11.8 %shard_map.146 = bf16[32,16,256]{2,1,0:T(8,128)(2,1)} custom-call(bf16[32,16,256]{2,1,0:T(8,128)(2,1)} %broadcast_in_dim.272.x_ref), custom_call_target="tpu_custom_call" | custom-call | tf_op jit(solution)/shard_map/pallas_call | solution.py:353
  108.5 1.9 broadcast_in_dim.280
  110.4 3.0 convert_element_type.126.mask_ref
  113.4 12.9 %shard_map.147 = (f32[8,256,128]{2,1,0:T(8,128)}, f32[8,256,128]{2,1,0:T(8,128)}, f32[8,256,128]{2,1,0:T(8,128)}) custom-call(bf16[8,256,128]{2,1,0:T(8,128)(2,1)} %broadcast_select_fusion.1.q_ref, bf16[2,2048,512]{2,1,0:T(8,128)(2,1)} %k_ref.3, bf16[2,2048,512]{2,1,0:T(8,128)(2,1)} %v_ref.3, f32[256,2048]{1,0:T(8,128)} %convert_element_type.126.mask_ref), custom_call_target="tpu_custom_call" | custom-call | tf_op jit(solution)/shard_map/pallas_call | solution.py:441
  126.4 2.1 slice_reduce_fusion.2
  132.0 15.6 %shard_map.148 = (bf16[32,16,256]{2,1,0:T(8,128)(2,1)}, f32[32,8,256]{2,1,0:T(8,128)}) custom-call(bf16[32,16,256]{2,1,0:T(8,128)(2,1)} %bitcast.173, f32[32,8,256]{2,1,0:T(8,128)} %maximum_maximum_fusion.xb_ref), custom_call_target="tpu_custom_call" | custom-call | tf_op jit(solution)/shard_map/pallas_call | solution.py:399
  151.7 1.8 fusion.31
  153.6 2.1 fusion
  157.1 35.0 %shard_map.149 = bf16[2,64,32,128]{3,2,1,0:T(8,128)(2,1)} custom-call(bf16[2,64,32,128]{3,2,1,0:T(8,128)(2,1)} %reshape.520.x_ref), custom_call_target="tpu_custom_call" | custom-call | tf_op jit(solution)/shard_map/pallas_call | solution.py:243
  192.1 1.9 fusion.8
  196.4 2.1 add_convert_fusion
  200.0 1.8 fusion.123
  203.0 12.0 %shard_map.150 = bf16[32,16,256]{2,1,0:T(8,128)(2,1)} custom-call(bf16[32,16,256]{2,1,0:T(8,128)(2,1)} %broadcast_in_dim.288.x_ref), custom_call_target="tpu_custom_call" | custom-call | tf_op jit(solution)/shard_map/pallas_call | solution.py:353
  218.7 12.9 %shard_map.151 = (f32[8,256,128]{2,1,0:T(8,128)}, f32[8,256,128]{2,1,0:T(8,128)}, f32[8,256,128]{2,1,0:T(8,128)}) custom-call(bf16[8,256,128]{2,1,0:T(8,128)(2,1)} %broadcast_select_fusion.q_ref, bf16[2,2048,512]{2,1,0:T(8,128)(2,1)} %k_ref.3, bf16[2,2048,512]{2,1,0:T(8,128)(2,1)} %v_ref.3, f32[256,2048]{1,0:T(8,128)} %convert_element_type.126.mask_ref), custom_call_target="tpu_custom_call" | custom-call | tf_op jit(solution)/shard_map/pallas_call | solution.py:441
  238.1 16.2 %shard_map.152 = (bf16[32,16,256]{2,1,0:T(8,128)(2,1)}, f32[32,8,256]{2,1,0:T(8,128)}) custom-call(bf16[32,16,256]{2,1,0:T(8,128)(2,1)} %bitcast.172, f32[32,8,256]{2,1,0:T(8,128)} %maximum_maximum_fusion.1.xb_ref), custom_call_target="tpu_custom_call" | custom-call | tf_op jit(solution)/shard_map/pallas_call | solution.py:399
  260.5 35.8 %shard_map.153 = bf16[2,64,32,128]{3,2,1,0:T(8,128)(2,1)} custom-call(bf16[2,64,32,128]{3,2,1,0:T(8,128)(2,1)} %reshape.529.x_ref), custom_call_target="tpu_custom_call" | custom-call | tf_op jit(solution)/shard_map/pallas_call | solution.py:243
  296.4 3.4 %convert_add_fusion.1 = f32[2,64,32,128]{3,2,1,0:T(8,128)} fusion(bf16[2,64,32,128]{3,2,1,0:T(8,128)(2,1)} %shard_map.153, bf16[2,64,32,128]{3,2,1,0:T(8,128)(2,1)} %shard_map.149, bf16[2,64,32,128]{3,2,1,0:T(8,128)(2,1)S(1)} %copy-done.2), kind=kLoop, calls=%fused_computation.14 | loop fusion | flops 2621440 | bytes 5242880 | tf_op jit(solution)/shard_map/add | solution.py:666
  299.8 2.9 add.280
  (210 shorter events, 49.1 us)
Async XLA Ops:
  0.0 1.4 copy-start
  2.8 0.9 copy-start.11
  2.8 3.8 %copy-start.6 = (bf16[2,64,3,512]{3,1,2,0:T(8,128)(2,1)S(1)}, bf16[2,64,3,512]{3,1,2,0:T(8,128)(2,1)}, u32[]{:S(2)}) copy-start(bf16[2,64,3,512]{3,1,2,0:T(8,128)(2,1)} %param.25) | copy-start | bytes 1179652
  6.6 1.2 copy-start.4
  75.5 2.5 copy-start.2
  75.5 4.3 %copy-start.8 = (f32[2,2048]{1,0:T(2,128)S(1)}, f32[2,2048]{1,0:T(2,128)}, u32[]{:S(2)}) copy-start(f32[2,2048]{1,0:T(2,128)} %param.23) | copy-start | bytes 49156
  75.5 4.4 %copy-start.9 = (f32[2,2048]{1,0:T(2,128)S(1)}, f32[2,2048]{1,0:T(2,128)}, u32[]{:S(2)}) copy-start(f32[2,2048]{1,0:T(2,128)} %param.24) | copy-start | bytes 49156
  90.0 0.7 copy-start.13
  90.0 0.7 copy-start.14
  90.0 0.8 copy-start.15
  92.2 15.7 %copy-start.12 = (s32[16,2]{0,1:T(2,128)S(1)}, s32[16,2]{0,1:T(2,128)}, u32[]{:S(2)}) copy-start(s32[16,2]{0,1:T(2,128)} %param.20) | copy-start | bytes 388
  131.1 20.6 %copy-start.7 = (bf16[2,16,2048]{2,1,0:T(8,128)(2,1)S(1)}, bf16[2,16,2048]{2,1,0:T(8,128)(2,1)}, u32[]{:S(2)}) copy-start(bf16[2,16,2048]{2,1,0:T(8,128)(2,1)} %param.28) | copy-start | bytes 393220
  147.6 5.9 %copy-start.10 = (f32[2,2048]{1,0:T(2,128)S(1)}, f32[2,2048]{1,0:T(2,128)}, u32[]{:S(2)}) copy-start(f32[2,2048]{1,0:T(2,128)} %param.27) | copy-start | bytes 49156
  147.6 6.0 %copy-start.5 = (bf16[2,64,2048]{2,1,0:T(8,128)(2,1)S(1)}, bf16[2,64,2048]{2,1,0:T(8,128)(2,1)}, u32[]{:S(2)}) copy-start(bf16[2,64,2048]{2,1,0:T(8,128)(2,1)} %param.29) | copy-start | bytes 1572868
  192.1 2.5 copy-start.3
  296.4 6.3 %copy-start.1 = (bf16[400,2048]{1,0:T(8,128)(2,1)S(1)}, bf16[400,2048]{1,0:T(8,128)(2,1)}, u32[]{:S(2)}) copy-start(bf16[400,2048]{1,0:T(8,128)(2,1)} %param.16) | copy-start | bytes 4915204

commit v4 on v3

--- a/solution.py
+++ b/solution.py
@@ -414,6 +414,85 @@
             collective_id=_kernel_id(("all_to_all_pair", whole, xa.shape, xb.shape)),
         ),
     )(xa, xb)
+
+
+def _gather_chip_kernel(x_ref, o_ref, buf, sx, sp, rr, sa):
+    seq_index = lax.axis_index("seq")
+    tp_index = lax.axis_index("tp")
+    count = buf.shape[0]
+    core = seq_index % 2
+    mate = seq_index + 1 - 2 * core
+    n = count // 2
+    me = seq_index // 2
+
+    def peer(m):
+        return (m * 2 + core, tp_index)
+
+    barrier = pltpu.get_barrier_semaphore()
+
+    def greet(i, carry):
+        m = lax.rem(me + i, n)
+        pl.semaphore_signal(barrier, 1, device_id=peer(m), device_id_type=MESH_IDS)
+        return carry
+
+    lax.fori_loop(1, n, greet, 0)
+    pl.semaphore_signal(barrier, 1, device_id=(mate, tp_index), device_id_type=MESH_IDS)
+    pl.semaphore_wait(barrier, n)
+
+    swap = _rcopy(x_ref, buf.at[seq_index], sa, rr.at[seq_index], (mate, tp_index))
+    swap.start()
+
+    def start_own(i, carry):
+        m = lax.rem(me + i, n)
+        _rcopy(x_ref, buf.at[seq_index], sx.at[m], rr.at[seq_index], peer(m)).start()
+        return carry
+
+    lax.fori_loop(1, n, start_own, 0)
+    _rcopy(x_ref, buf.at[mate], sa, rr.at[mate], (mate, tp_index)).wait_recv()
+
+    def start_mate(i, carry):
+        m = lax.rem(me + i, n)
+        _rcopy(buf.at[mate], buf.at[mate], sp.at[m], rr.at[mate], peer(m)).start()
+        return carry
+
+    lax.fori_loop(1, n, start_mate, 0)
+
+    def finish(i, carry):
+        m = lax.rem(me + i, n)
+        j = m * 2 + core
+        k = m * 2 + 1 - core
+        _rcopy(x_ref, buf.at[j], sx.at[m], rr.at[j], peer(m)).wait_recv()
+        _rcopy(x_ref, buf.at[k], sp.at[m], rr.at[k], peer(m)).wait_recv()
+        _rcopy(x_ref, buf.at[seq_index], sx.at[m], rr.at[seq_index], peer(m)).wait_send()
+        _rcopy(buf.at[mate], buf.at[mate], sp.at[m], rr.at[mate], peer(m)).wait_send()
+        return carry
+
+    lax.fori_loop(1, n, finish, 0)
+    swap.wait_send()
+    buf[seq_index] = x_ref[...]
+    o_ref[...] = buf[...]
+
+
+def gather_chip(x, count):
+    shape = (count,) + x.shape
+    n = count // 2
+    return pl.pallas_call(
+        _gather_chip_kernel,
+        out_shape=jax.ShapeDtypeStruct(shape, x.dtype),
+        in_specs=[pl.BlockSpec(memory_space=pltpu.VMEM)],
+        out_specs=pl.BlockSpec(memory_space=pltpu.VMEM),
+        scratch_shapes=[
+            pltpu.VMEM(shape, x.dtype),
+            pltpu.SemaphoreType.DMA((n,)),
+            pltpu.SemaphoreType.DMA((n,)),
+            pltpu.SemaphoreType.DMA((count,)),
+            pltpu.SemaphoreType.DMA(()),
+        ],
+        compiler_params=pltpu.CompilerParams(
+            has_side_effects=True,
+            collective_id=_kernel_id(("gather_chip", shape, str(x.dtype))),
+        ),
+    )(x)
 
 
 def _attention_kernel(scale, q_ref, k_ref, v_ref, mask_ref, o_ref, m_ref, l_ref):
@@ -588,7 +667,7 @@
             ]
         )
         activated = jax.nn.gelu(pre_act, approximate=True).astype(jnp.bfloat16)
-        q_all = all_to_all(jnp.broadcast_to(q_piece[None], (seq_count,) + q_piece.shape), False, tp_count)
+        q_all = gather_chip(q_piece, seq_count)
         queries = (
             q_all.reshape(heads_local, pieces, sub_width, rows)
             .transpose(3, 0, 1, 2)

time: 305 us -> 304 us (level)
  no operation moved by 1% of the time
where the time goes in v4:
time: 304 us; the launch traced here: 302 us
  Pallas kernels  216 us (71%)
  local copies, waits for them, and re-layouts  47.7 us (16%)
  other arithmetic  29.1 us (10%)
  matrix products  8.05 us (3%)
    pallas_call x2, Pallas kernels, allreduce_chip(): pl.pallas_call(functools.partial(_allreduce_chip_kernel, tp_count), out_s...  70.6 us
    pallas_call x1, Pallas kernels, opening(): pl.pallas_call(functools.partial(_opening_kernel, tp_count), out_shape=(j...  64.3 us
    pallas_call x2, Pallas kernels, all_to_all_pair(): pl.pallas_call(functools.partial(_all_to_all_pair_kernel, n, whole, tp_co...  32.8 us
    pallas_call x2, Pallas kernels, cache_attention(): pl.pallas_call(functools.partial(_attention_kernel, scale), grid=(heads /...  25.9 us
    pallas_call x2, Pallas kernels, gather_chip(): pl.pallas_call(_gather_chip_kernel, out_shape=jax.ShapeDtypeStruct(shape,...  22.2 us

profile of v4, /device:TPU:25, one launch (start us, length us, event | category | flops | bytes accessed | tf_op | source)
XLA Modules:
  0.0 301.6 jit_solution(12733891114504367827)
XLA Ops:
  4.2 2.4 select_select_fusion.x_ref
  11.2 64.3 %shard_map.145 = (bf16[2,64,32,128]{3,2,1,0:T(8,128)(2,1)}, bf16[32,176,128]{2,1,0:T(8,128)(2,1)}) custom-call(bf16[2,64,32,128]{3,2,1,0:T(8,128)(2,1)} %select_select_fusion.x_ref, bf16[32,176,128]{2,1,0:T(8,128)(2,1)} %pad_maximum_fusion.w_ref), custom_call_target="tpu_custom_call" | custom-call | tf_op jit(solution)/shard_map/pallas_call | solution.py:300
  75.5 1.9 convert_reduce_fusion
  79.9 2.1 fusion.7
  83.5 3.8 %copy.193 = bf16[32,176,128]{1,2,0:T(8,128)(2,1)} copy(bf16[32,176,128]{2,1,0:T(8,128)(2,1)} %get-tuple-element.18) | data formatting | bytes 2883584 | tf_op jit(solution)/shard_map/pallas_call | solution.py:300
  87.3 2.7 fusion.115
  92.1 10.8 %shard_map.146 = bf16[32,16,256]{2,1,0:T(8,128)(2,1)} custom-call(bf16[16,256]{1,0:T(8,128)(2,1)} %fusion.95.x_ref), custom_call_target="tpu_custom_call" | custom-call | tf_op jit(solution)/shard_map/pallas_call | solution.py:479
  107.4 1.9 broadcast_in_dim.267
  109.3 3.0 convert_element_type.126.mask_ref
  112.3 12.9 %shard_map.147 = (f32[8,256,128]{2,1,0:T(8,128)}, f32[8,256,128]{2,1,0:T(8,128)}, f32[8,256,128]{2,1,0:T(8,128)}) custom-call(bf16[8,256,128]{2,1,0:T(8,128)(2,1)} %broadcast_select_fusion.1.q_ref, bf16[2,2048,512]{2,1,0:T(8,128)(2,1)} %k_ref.3, bf16[2,2048,512]{2,1,0:T(8,128)(2,1)} %v_ref.3, f32[256,2048]{1,0:T(8,128)} %convert_element_type.126.mask_ref), custom_call_target="tpu_custom_call" | custom-call | tf_op jit(solution)/shard_map/pallas_call | solution.py:520
  125.2 2.1 slice_reduce_fusion.2
  130.8 16.3 %shard_map.148 = (bf16[32,16,256]{2,1,0:T(8,128)(2,1)}, f32[32,8,256]{2,1,0:T(8,128)}) custom-call(bf16[32,16,256]{2,1,0:T(8,128)(2,1)} %bitcast.173, f32[32,8,256]{2,1,0:T(8,128)} %maximum_maximum_fusion.xb_ref), custom_call_target="tpu_custom_call" | custom-call | tf_op jit(solution)/shard_map/pallas_call | solution.py:399
  151.3 1.8 fusion.31
  153.2 2.1 fusion
  156.6 35.0 %shard_map.149 = bf16[2,64,32,128]{3,2,1,0:T(8,128)(2,1)} custom-call(bf16[2,64,32,128]{3,2,1,0:T(8,128)(2,1)} %reshape.518.x_ref), custom_call_target="tpu_custom_call" | custom-call | tf_op jit(solution)/shard_map/pallas_call | solution.py:243
  191.6 1.9 fusion.8
  196.0 2.1 add_convert_fusion
  199.6 1.8 fusion.123
  202.4 11.4 %shard_map.150 = bf16[32,16,256]{2,1,0:T(8,128)(2,1)} custom-call(bf16[16,256]{1,0:T(8,128)(2,1)} %fusion.96.x_ref), custom_call_target="tpu_custom_call" | custom-call | tf_op jit(solution)/shard_map/pallas_call | solution.py:479
  217.5 12.9 %shard_map.151 = (f32[8,256,128]{2,1,0:T(8,128)}, f32[8,256,128]{2,1,0:T(8,128)}, f32[8,256,128]{2,1,0:T(8,128)}) custom-call(bf16[8,256,128]{2,1,0:T(8,128)(2,1)} %broadcast_select_fusion.q_ref, bf16[2,2048,512]{2,1,0:T(8,128)(2,1)} %k_ref.3, bf16[2,2048,512]{2,1,0:T(8,128)(2,1)} %v_ref.3, f32[256,2048]{1,0:T(8,128)} %convert_element_type.126.mask_ref), custom_call_target="tpu_custom_call" | custom-call | tf_op jit(solution)/shard_map/pallas_call | solution.py:520
  236.9 16.4 %shard_map.152 = (bf16[32,16,256]{2,1,0:T(8,128)(2,1)}, f32[32,8,256]{2,1,0:T(8,128)}) custom-call(bf16[32,16,256]{2,1,0:T(8,128)(2,1)} %bitcast.172, f32[32,8,256]{2,1,0:T(8,128)} %maximum_maximum_fusion.1.xb_ref), custom_call_target="tpu_custom_call" | custom-call | tf_op jit(solution)/shard_map/pallas_call | solution.py:399
  259.6 35.6 %shard_map.153 = bf16[2,64,32,128]{3,2,1,0:T(8,128)(2,1)} custom-call(bf16[2,64,32,128]{3,2,1,0:T(8,128)(2,1)} %reshape.527.x_ref), custom_call_target="tpu_custom_call" | custom-call | tf_op jit(solution)/shard_map/pallas_call | solution.py:243
  295.3 3.4 %convert_add_fusion.1 = f32[2,64,32,128]{3,2,1,0:T(8,128)} fusion(bf16[2,64,32,128]{3,2,1,0:T(8,128)(2,1)} %shard_map.153, bf16[2,64,32,128]{3,2,1,0:T(8,128)(2,1)} %shard_map.149, bf16[2,64,32,128]{3,2,1,0:T(8,128)(2,1)S(1)} %copy-done.2), kind=kLoop, calls=%fused_computation.14 | loop fusion | flops 2621440 | bytes 5242880 | tf_op jit(solution)/shard_map/add | solution.py:745
  298.8 2.9 add.280
  (208 shorter events, 48.9 us)
Async XLA Ops:
  0.0 1.4 copy-start
  2.8 0.9 copy-start.11
  2.8 3.8 %copy-start.6 = (bf16[2,64,3,512]{3,1,2,0:T(8,128)(2,1)S(1)}, bf16[2,64,3,512]{3,1,2,0:T(8,128)(2,1)}, u32[]{:S(2)}) copy-start(bf16[2,64,3,512]{3,1,2,0:T(8,128)(2,1)} %param.25) | copy-start | bytes 1179652
  6.6 1.2 copy-start.4
  75.5 2.5 copy-start.2
  75.5 4.3 %copy-start.8 = (f32[2,2048]{1,0:T(2,128)S(1)}, f32[2,2048]{1,0:T(2,128)}, u32[]{:S(2)}) copy-start(f32[2,2048]{1,0:T(2,128)} %param.23) | copy-start | bytes 49156
  75.5 4.4 %copy-start.9 = (f32[2,2048]{1,0:T(2,128)S(1)}, f32[2,2048]{1,0:T(2,128)}, u32[]{:S(2)}) copy-start(f32[2,2048]{1,0:T(2,128)} %param.24) | copy-start | bytes 49156
  90.0 0.7 copy-start.13
  90.0 0.7 copy-start.14
  90.0 0.8 copy-start.15
  91.1 15.7 %copy-start.12 = (s32[16,2]{0,1:T(2,128)S(1)}, s32[16,2]{0,1:T(2,128)}, u32[]{:S(2)}) copy-start(s32[16,2]{0,1:T(2,128)} %param.20) | copy-start | bytes 388
  130.0 21.3 %copy-start.7 = (bf16[2,16,2048]{2,1,0:T(8,128)(2,1)S(1)}, bf16[2,16,2048]{2,1,0:T(8,128)(2,1)}, u32[]{:S(2)}) copy-start(bf16[2,16,2048]{2,1,0:T(8,128)(2,1)} %param.28) | copy-start | bytes 393220
  147.2 5.9 %copy-start.10 = (f32[2,2048]{1,0:T(2,128)S(1)}, f32[2,2048]{1,0:T(2,128)}, u32[]{:S(2)}) copy-start(f32[2,2048]{1,0:T(2,128)} %param.27) | copy-start | bytes 49156
  147.2 6.0 %copy-start.5 = (bf16[2,64,2048]{2,1,0:T(8,128)(2,1)S(1)}, bf16[2,64,2048]{2,1,0:T(8,128)(2,1)}, u32[]{:S(2)}) copy-start(bf16[2,64,2048]{2,1,0:T(8,128)(2,1)} %param.29) | copy-start | bytes 1572868
  191.6 2.5 copy-start.3
  295.3 6.3 %copy-start.1 = (bf16[400,2048]{1,0:T(8,128)(2,1)S(1)}, bf16[400,2048]{1,0:T(8,128)(2,1)}, u32[]{:S(2)}) copy-start(bf16[400,2048]{1,0:T(8,128)(2,1)} %param.16) | copy-start | bytes 4915204

commit v5 on v4

--- a/solution.py
+++ b/solution.py
@@ -586,7 +586,7 @@
     own_prompt = seg_slot[None, :] == group_of[:, None]
     allowed = (own_tail | own_prompt) & live_slot[None, :]
     allowed = jnp.repeat(allowed, new_tokens, axis=0)
-    mask_f = allowed.astype(jnp.float32)
+    mask_f = allowed.astype(jnp.bfloat16)
 
     rows_local = w_qkv.shape[1]
     unit_count = w_fc2.shape[1]

time: 304 us -> 300 us (0.987)
  local copies, waits for them, and re-layouts: 47.7 us -> 44.5 us
where the time goes in v5:
time: 300 us; the launch traced here: 297 us
  Pallas kernels  215 us (72%)
  local copies, waits for them, and re-layouts  44.5 us (15%)
  other arithmetic  29.1 us (10%)
  matrix products  8.05 us (3%)
    pallas_call x2, Pallas kernels, allreduce_chip(): pl.pallas_call(functools.partial(_allreduce_chip_kernel, tp_count), out_s...  70.6 us
    pallas_call x1, Pallas kernels, opening(): pl.pallas_call(functools.partial(_opening_kernel, tp_count), out_shape=(j...  64.3 us
    pallas_call x2, Pallas kernels, all_to_all_pair(): pl.pallas_call(functools.partial(_all_to_all_pair_kernel, n, whole, tp_co...  32.8 us
    pallas_call x2, Pallas kernels, cache_attention(): pl.pallas_call(functools.partial(_attention_kernel, scale), grid=(heads /...  24.9 us
    pallas_call x2, Pallas kernels, gather_chip(): pl.pallas_call(_gather_chip_kernel, out_shape=jax.ShapeDtypeStruct(shape,...  22.2 us

profile of v5, /device:TPU:25, one launch (start us, length us, event | category | flops | bytes accessed | tf_op | source)
XLA Modules:
  0.0 297.4 jit_solution(16127537361900670819)
XLA Ops:
  4.2 2.4 select_select_fusion.x_ref
  11.2 64.3 %shard_map.145 = (bf16[2,64,32,128]{3,2,1,0:T(8,128)(2,1)}, bf16[32,176,128]{2,1,0:T(8,128)(2,1)}) custom-call(bf16[2,64,32,128]{3,2,1,0:T(8,128)(2,1)} %select_select_fusion.x_ref, bf16[32,176,128]{2,1,0:T(8,128)(2,1)} %pad_maximum_fusion.w_ref), custom_call_target="tpu_custom_call" | custom-call | tf_op jit(solution)/shard_map/pallas_call | solution.py:300
  75.5 1.9 convert_reduce_fusion
  79.9 2.1 fusion.7
  83.5 3.8 %copy.193 = bf16[32,176,128]{1,2,0:T(8,128)(2,1)} copy(bf16[32,176,128]{2,1,0:T(8,128)(2,1)} %get-tuple-element.18) | data formatting | bytes 2883584 | tf_op jit(solution)/shard_map/pallas_call | solution.py:300
  87.3 2.8 fusion.115
  92.1 10.8 %shard_map.146 = bf16[32,16,256]{2,1,0:T(8,128)(2,1)} custom-call(bf16[16,256]{1,0:T(8,128)(2,1)} %fusion.95.x_ref), custom_call_target="tpu_custom_call" | custom-call | tf_op jit(solution)/shard_map/pallas_call | solution.py:479
  109.1 12.4 %shard_map.147 = (f32[8,256,128]{2,1,0:T(8,128)}, f32[8,256,128]{2,1,0:T(8,128)}, f32[8,256,128]{2,1,0:T(8,128)}) custom-call(bf16[8,256,128]{2,1,0:T(8,128)(2,1)} %broadcast_select_fusion.1.q_ref, bf16[2,2048,512]{2,1,0:T(8,128)(2,1)} %k_ref.3, bf16[2,2048,512]{2,1,0:T(8,128)(2,1)} %v_ref.3, bf16[256,2048]{1,0:T(8,128)(2,1)} %convert_element_type.126.mask_ref), custom_call_target="tpu_custom_call" | custom-call | tf_op jit(solution)/shard_map/pallas_call | solution.py:520
  121.5 2.1 slice_reduce_fusion.2
  127.1 16.3 %shard_map.148 = (bf16[32,16,256]{2,1,0:T(8,128)(2,1)}, f32[32,8,256]{2,1,0:T(8,128)}) custom-call(bf16[32,16,256]{2,1,0:T(8,128)(2,1)} %bitcast.173, f32[32,8,256]{2,1,0:T(8,128)} %maximum_maximum_fusion.xb_ref), custom_call_target="tpu_custom_call" | custom-call | tf_op jit(solution)/shard_map/pallas_call | solution.py:399
  147.6 1.8 fusion.31
  149.5 2.1 fusion
  152.9 35.0 %shard_map.149 = bf16[2,64,32,128]{3,2,1,0:T(8,128)(2,1)} custom-call(bf16[2,64,32,128]{3,2,1,0:T(8,128)(2,1)} %reshape.518.x_ref), custom_call_target="tpu_custom_call" | custom-call | tf_op jit(solution)/shard_map/pallas_call | solution.py:243
  187.9 1.9 fusion.8
  192.3 2.1 add_convert_fusion
  195.9 1.8 fusion.123
  198.7 11.4 %shard_map.150 = bf16[32,16,256]{2,1,0:T(8,128)(2,1)} custom-call(bf16[16,256]{1,0:T(8,128)(2,1)} %fusion.96.x_ref), custom_call_target="tpu_custom_call" | custom-call | tf_op jit(solution)/shard_map/pallas_call | solution.py:479
  213.8 12.4 %shard_map.151 = (f32[8,256,128]{2,1,0:T(8,128)}, f32[8,256,128]{2,1,0:T(8,128)}, f32[8,256,128]{2,1,0:T(8,128)}) custom-call(bf16[8,256,128]{2,1,0:T(8,128)(2,1)} %broadcast_select_fusion.q_ref, bf16[2,2048,512]{2,1,0:T(8,128)(2,1)} %k_ref.3, bf16[2,2048,512]{2,1,0:T(8,128)(2,1)} %v_ref.3, bf16[256,2048]{1,0:T(8,128)(2,1)} %convert_element_type.126.mask_ref), custom_call_target="tpu_custom_call" | custom-call | tf_op jit(solution)/shard_map/pallas_call | solution.py:520
  226.2 1.6 slice_reduce_fusion.1
  227.8 1.6 slice_reduce_fusion
  232.7 16.4 %shard_map.152 = (bf16[32,16,256]{2,1,0:T(8,128)(2,1)}, f32[32,8,256]{2,1,0:T(8,128)}) custom-call(bf16[32,16,256]{2,1,0:T(8,128)(2,1)} %bitcast.172, f32[32,8,256]{2,1,0:T(8,128)} %maximum_maximum_fusion.1.xb_ref), custom_call_target="tpu_custom_call" | custom-call | tf_op jit(solution)/shard_map/pallas_call | solution.py:399
  255.4 35.6 %shard_map.153 = bf16[2,64,32,128]{3,2,1,0:T(8,128)(2,1)} custom-call(bf16[2,64,32,128]{3,2,1,0:T(8,128)(2,1)} %reshape.527.x_ref), custom_call_target="tpu_custom_call" | custom-call | tf_op jit(solution)/shard_map/pallas_call | solution.py:243
  291.1 3.4 %convert_add_fusion.1 = f32[2,64,32,128]{3,2,1,0:T(8,128)} fusion(bf16[2,64,32,128]{3,2,1,0:T(8,128)(2,1)} %shard_map.153, bf16[2,64,32,128]{3,2,1,0:T(8,128)(2,1)} %shard_map.149, bf16[2,64,32,128]{3,2,1,0:T(8,128)(2,1)S(1)} %copy-done.2), kind=kLoop, calls=%fused_computation.14 | loop fusion | flops 2621440 | bytes 5242880 | tf_op jit(solution)/shard_map/add | solution.py:745
  294.5 2.9 add.280
  (208 shorter events, 47.4 us)
Async XLA Ops:
  0.0 1.4 copy-start
  2.8 0.9 copy-start.11
  2.8 3.8 %copy-start.6 = (bf16[2,64,3,512]{3,1,2,0:T(8,128)(2,1)S(1)}, bf16[2,64,3,512]{3,1,2,0:T(8,128)(2,1)}, u32[]{:S(2)}) copy-start(bf16[2,64,3,512]{3,1,2,0:T(8,128)(2,1)} %param.25) | copy-start | bytes 1179652
  6.6 1.2 copy-start.4
  75.5 2.5 copy-start.2
  75.5 4.3 %copy-start.8 = (f32[2,2048]{1,0:T(2,128)S(1)}, f32[2,2048]{1,0:T(2,128)}, u32[]{:S(2)}) copy-start(f32[2,2048]{1,0:T(2,128)} %param.23) | copy-start | bytes 49156
  75.5 4.4 %copy-start.9 = (f32[2,2048]{1,0:T(2,128)S(1)}, f32[2,2048]{1,0:T(2,128)}, u32[]{:S(2)}) copy-start(f32[2,2048]{1,0:T(2,128)} %param.24) | copy-start | bytes 49156
  90.1 0.7 copy-start.13
  90.1 0.7 copy-start.14
  90.1 0.8 copy-start.15
  91.2 15.7 %copy-start.12 = (s32[16,2]{0,1:T(2,128)S(1)}, s32[16,2]{0,1:T(2,128)}, u32[]{:S(2)}) copy-start(s32[16,2]{0,1:T(2,128)} %param.20) | copy-start | bytes 388
  126.3 21.3 %copy-start.7 = (bf16[2,16,2048]{2,1,0:T(8,128)(2,1)S(1)}, bf16[2,16,2048]{2,1,0:T(8,128)(2,1)}, u32[]{:S(2)}) copy-start(bf16[2,16,2048]{2,1,0:T(8,128)(2,1)} %param.28) | copy-start | bytes 393220
  143.5 5.9 %copy-start.10 = (f32[2,2048]{1,0:T(2,128)S(1)}, f32[2,2048]{1,0:T(2,128)}, u32[]{:S(2)}) copy-start(f32[2,2048]{1,0:T(2,128)} %param.27) | copy-start | bytes 49156
  143.5 6.0 %copy-start.5 = (bf16[2,64,2048]{2,1,0:T(8,128)(2,1)S(1)}, bf16[2,64,2048]{2,1,0:T(8,128)(2,1)}, u32[]{:S(2)}) copy-start(bf16[2,64,2048]{2,1,0:T(8,128)(2,1)} %param.29) | copy-start | bytes 1572868
  187.9 2.5 copy-start.3
  291.0 6.3 %copy-start.1 = (bf16[400,2048]{1,0:T(8,128)(2,1)S(1)}, bf16[400,2048]{1,0:T(8,128)(2,1)}, u32[]{:S(2)}) copy-start(bf16[400,2048]{1,0:T(8,128)(2,1)} %param.16) | copy-start | bytes 4915204

commit v6 on v5

--- a/solution.py
+++ b/solution.py
@@ -505,9 +505,10 @@
         top = jnp.max(scores, axis=1, keepdims=True)
         weights = jnp.where(valid, jnp.exp(scores - top), 0.0)
         total = jnp.sum(weights, axis=1, keepdims=True)
-        o_ref[half] = jnp.dot(
+        weighted = jnp.dot(
             weights.astype(jnp.bfloat16), v_ref[...], preferred_element_type=jnp.float32
         )
+        o_ref[half] = weighted[:, half * HEAD_DIM : (half + 1) * HEAD_DIM]
         m_ref[half] = jnp.broadcast_to(top, m_ref.shape[1:])
         l_ref[half] = jnp.broadcast_to(total, l_ref.shape[1:])
 
@@ -520,14 +521,15 @@
     return pl.pallas_call(
         functools.partial(_attention_kernel, scale),
         grid=(heads // per_block,),
-        out_shape=[jax.ShapeDtypeStruct((heads, rows, lanes), jnp.float32)] * 3,
+        out_shape=[jax.ShapeDtypeStruct((heads, rows, HEAD_DIM), jnp.float32)]
+        + [jax.ShapeDtypeStruct((heads, rows, lanes), jnp.float32)] * 2,
         in_specs=[
             pl.BlockSpec((per_block, rows, lanes), lambda b: (b, 0, 0)),
             pl.BlockSpec((None, slots, lanes), lambda b: (layer_index, 0, b)),
             pl.BlockSpec((None, slots, lanes), lambda b: (layer_index, 0, b)),
             pl.BlockSpec((rows, slots), lambda b: (0, 0)),
         ],
-        out_specs=[out_spec] * 3,
+        out_specs=[pl.BlockSpec((per_block, rows, HEAD_DIM), lambda b: (b, 0, 0))] + [out_spec] * 2,
     )(q_pad, k_cache, v_cache, mask)
 
 
@@ -685,14 +687,7 @@
         out_pad, max_pad, sum_pad = cache_attention(
             q_pad, k_cache, v_cache, mask_f, layer_index, score_scale
         )
-        part_out = jnp.sum(
-            jnp.where(
-                same_half[None, :, None, :, None],
-                out_pad.reshape(heads_local // per_block, per_block, rows, per_block, HEAD_DIM),
-                0.0,
-            ),
-            axis=3,
-        ).reshape(heads_local, rows, HEAD_DIM)
+        part_out = out_pad
         part_max = max_pad[:, :, 0]
         part_sum = sum_pad[:, :, 0]
         out_pieces = (

time: 300 us -> 330 us (1.10)
  local copies, waits for them, and re-layouts: 44.5 us -> 59 us
  other arithmetic: 29.1 us -> 37.2 us
  matrix products: 8.05 us -> 13.7 us
    broadcast_in_dim x4 -> x6, local copies, waits for them, and re-layouts: 2.54 us -> 6.38 us  [per_device(): jnp.where(same_half[None, :, None, :, None], q_pairs[:, :, :, None, :], j...]
where the time goes in v6:
time: 330 us; the launch traced here: 327 us
  Pallas kernels  216 us (65%)
  local copies, waits for them, and re-layouts  59 us (18%)
  other arithmetic  37.2 us (11%)
  matrix products  13.7 us (4%)
    pallas_call x2, Pallas kernels, allreduce_chip(): pl.pallas_call(functools.partial(_allreduce_chip_kernel, tp_count), out_s...  70.6 us
    pallas_call x1, Pallas kernels, opening(): pl.pallas_call(functools.partial(_opening_kernel, tp_count), out_shape=(j...  64.3 us
    pallas_call x2, Pallas kernels, all_to_all_pair(): pl.pallas_call(functools.partial(_all_to_all_pair_kernel, n, whole, tp_co...  32.8 us
    pallas_call x2, Pallas kernels, cache_attention(): pl.pallas_call(functools.partial(_attention_kernel, scale), grid=(heads /...  25.7 us
    pallas_call x2, Pallas kernels, gather_chip(): pl.pallas_call(_gather_chip_kernel, out_shape=jax.ShapeDtypeStruct(shape,...  22.2 us

profile of v6, /device:TPU:25, one launch (start us, length us, event | category | flops | bytes accessed | tf_op | source)
XLA Modules:
  0.0 326.5 jit_solution(3296139370922760161)
XLA Ops:
  4.9 4.0 %select_select_fusion.x_ref = bf16[2,64,32,128]{3,2,1,0:T(8,128)(2,1)} fusion(bf16[2,64,32,128]{3,2,1,0:T(8,128)(2,1)} %gather.7, pred[2,64,32]{2,1,0:T(8,128)(4,1)S(1)} %copy.185, pred[2,64,32]{2,1,0:T(8,128)(4,1)S(1)} %copy.182), kind=kLoop, calls=%fused_computation.23 | loop fusion | flops 1048576 | bytes 2105344 | tf_op jit(solution)/shard_map/jit(_where)/select_n | solution.py:571
  14.8 2.3 pad_maximum_fusion.w_ref
  17.0 64.3 %shard_map.145 = (bf16[2,64,32,128]{3,2,1,0:T(8,128)(2,1)}, bf16[32,176,128]{2,1,0:T(8,128)(2,1)}) custom-call(bf16[2,64,32,128]{3,2,1,0:T(8,128)(2,1)} %select_select_fusion.x_ref, bf16[32,176,128]{2,1,0:T(8,128)(2,1)} %pad_maximum_fusion.w_ref), custom_call_target="tpu_custom_call" | custom-call | tf_op jit(solution)/shard_map/pallas_call | solution.py:300
  87.8 2.3 convert_element_type.121
  90.1 3.8 %copy.195 = bf16[32,176,128]{1,2,0:T(8,128)(2,1)} copy(bf16[32,176,128]{2,1,0:T(8,128)(2,1)} %get-tuple-element.18) | data formatting | bytes 2883584 | tf_op jit(solution)/shard_map/pallas_call | solution.py:300
  93.8 2.9 fusion.115
  98.8 10.8 %shard_map.146 = bf16[32,16,256]{2,1,0:T(8,128)(2,1)} custom-call(bf16[16,256]{1,0:T(8,128)(2,1)} %fusion.95.x_ref), custom_call_target="tpu_custom_call" | custom-call | tf_op jit(solution)/shard_map/pallas_call | solution.py:479
  117.4 2.2 convert_element_type.126.mask_ref
  119.6 12.9 %shard_map.147 = (f32[8,256,64]{2,1,0:T(8,128)}, f32[8,256,128]{2,1,0:T(8,128)}, f32[8,256,128]{2,1,0:T(8,128)}) custom-call(bf16[8,256,128]{2,1,0:T(8,128)(2,1)} %broadcast_select_fusion.1.q_ref, bf16[2,2048,512]{2,1,0:T(8,128)(2,1)} %k_ref.3, bf16[2,2048,512]{2,1,0:T(8,128)(2,1)} %v_ref.3, bf16[256,2048]{1,0:T(8,128)(2,1)} %convert_element_type.126.mask_ref), custom_call_target="tpu_custom_call" | custom-call | tf_op jit(solution)/shard_map/pallas_call | solution.py:521
  137.9 16.3 %shard_map.148 = (bf16[32,16,256]{2,1,0:T(8,128)(2,1)}, f32[32,8,256]{2,1,0:T(8,128)}) custom-call(bf16[32,16,256]{2,1,0:T(8,128)(2,1)} %bitcast.168, f32[32,8,256]{2,1,0:T(8,128)} %maximum_maximum_fusion.xb_ref), custom_call_target="tpu_custom_call" | custom-call | tf_op jit(solution)/shard_map/pallas_call | solution.py:399
  161.9 2.6 fusion.31
  165.1 3.1 fusion
  168.2 2.3 reshape.513.x_ref
  170.6 35.0 %shard_map.149 = bf16[2,64,32,128]{3,2,1,0:T(8,128)(2,1)} custom-call(bf16[2,64,32,128]{3,2,1,0:T(8,128)(2,1)} %reshape.513.x_ref), custom_call_target="tpu_custom_call" | custom-call | tf_op jit(solution)/shard_map/pallas_call | solution.py:243
  208.0 2.3 multiply_reduce_fusion
  210.9 3.8 %add_convert_fusion = bf16[2,64,32,128]{3,2,1,0:T(8,128)(2,1)} fusion(bf16[2,64,32,128]{3,2,1,0:T(8,128)(2,1)} %shard_map.149, bf16[2,64,32,128]{3,2,1,0:T(8,128)(2,1)S(1)} %copy-done.1, f32[32,128]{1,0:T(8,128)S(1)} %bitcast.188, f32[32,128]{1,0:T(8,128)S(1)} %bitcast.186, f32[2,64,32]{2,1,0:T(8,128)S(1)} %copy.210, f32[2,64,32]{2,1,0:T(8,128)S(1)} %copy.208), kind=kLoop, calls=%fused_computation.15 | loop fusion | flops 4194304 | bytes 3211264 | tf_op jit(solution)/shard_map/convert_element_type | solution.py:646
  214.6 2.3 convert_element_type.139
  220.1 11.4 %shard_map.150 = bf16[32,16,256]{2,1,0:T(8,128)(2,1)} custom-call(bf16[16,256]{1,0:T(8,128)(2,1)} %fusion.96.x_ref), custom_call_target="tpu_custom_call" | custom-call | tf_op jit(solution)/shard_map/pallas_call | solution.py:479
  237.0 12.7 %shard_map.151 = (f32[8,256,64]{2,1,0:T(8,128)}, f32[8,256,128]{2,1,0:T(8,128)}, f32[8,256,128]{2,1,0:T(8,128)}) custom-call(bf16[8,256,128]{2,1,0:T(8,128)(2,1)} %broadcast_select_fusion.q_ref, bf16[2,2048,512]{2,1,0:T(8,128)(2,1)} %k_ref.3, bf16[2,2048,512]{2,1,0:T(8,128)(2,1)} %v_ref.3, bf16[256,2048]{1,0:T(8,128)(2,1)} %convert_element_type.126.mask_ref), custom_call_target="tpu_custom_call" | custom-call | tf_op jit(solution)/shard_map/pallas_call | solution.py:521
  256.0 16.4 %shard_map.152 = (bf16[32,16,256]{2,1,0:T(8,128)(2,1)}, f32[32,8,256]{2,1,0:T(8,128)}) custom-call(bf16[32,16,256]{2,1,0:T(8,128)(2,1)} %bitcast.169, f32[32,8,256]{2,1,0:T(8,128)} %maximum_maximum_fusion.1.xb_ref), custom_call_target="tpu_custom_call" | custom-call | tf_op jit(solution)/shard_map/pallas_call | solution.py:399
  282.3 2.3 reshape.521.x_ref
  284.6 35.7 %shard_map.153 = bf16[2,64,32,128]{3,2,1,0:T(8,128)(2,1)} custom-call(bf16[2,64,32,128]{3,2,1,0:T(8,128)(2,1)} %reshape.521.x_ref), custom_call_target="tpu_custom_call" | custom-call | tf_op jit(solution)/shard_map/pallas_call | solution.py:243
  320.3 3.3 %convert_add_fusion.1 = f32[2,64,32,128]{3,2,1,0:T(8,128)} fusion(bf16[2,64,32,128]{3,2,1,0:T(8,128)(2,1)} %shard_map.153, bf16[2,64,32,128]{3,2,1,0:T(8,128)(2,1)} %shard_map.149, bf16[2,64,32,128]{3,2,1,0:T(8,128)(2,1)S(1)} %copy-done.1), kind=kLoop, calls=%fused_computation.14 | loop fusion | flops 2621440 | bytes 5242880 | tf_op jit(solution)/shard_map/add | solution.py:740
  323.6 2.9 add.280
  (232 shorter events, 67.6 us)
Async XLA Ops:
  0.0 1.4 copy-start
  2.8 1.7 copy-start.18
  2.8 6.1 %copy-start.7 = (bf16[2,64,3,512]{3,1,2,0:T(8,128)(2,1)S(1)}, bf16[2,64,3,512]{3,1,2,0:T(8,128)(2,1)}, u32[]{:S(2)}) copy-start(bf16[2,64,3,512]{3,1,2,0:T(8,128)(2,1)} %param.25) | copy-start | bytes 1179652
  81.3 2.5 copy-start.1
  81.3 4.3 %copy-start.11 = (f32[2,2048]{1,0:T(2,128)S(1)}, f32[2,2048]{1,0:T(2,128)}, u32[]{:S(2)}) copy-start(f32[2,2048]{1,0:T(2,128)} %param.23) | copy-start | bytes 49156
  81.3 4.4 %copy-start.12 = (f32[2,2048]{1,0:T(2,128)S(1)}, f32[2,2048]{1,0:T(2,128)}, u32[]{:S(2)}) copy-start(f32[2,2048]{1,0:T(2,128)} %param.24) | copy-start | bytes 49156
  93.8 2.9 copy-start.2
  97.6 17.7 %copy-start.8 = (f32[256]{0:T(256)}, f32[256]{0:T(256)S(1)}, u32[]{:S(2)}) copy-start(f32[256]{0:T(256)S(1)} %convert_element_type.123) | copy-start | bytes 3076
  97.7 16.7 %copy-start.16 = (f32[16]{0:T(128)}, f32[16]{0:T(128)S(1)}, u32[]{:S(2)}) copy-start(f32[16]{0:T(128)S(1)} %multiply_exponential_fusion) | copy-start | bytes 196
  97.8 17.5 %copy-start.24 = (s32[16,2]{0,1:T(2,128)S(1)}, s32[16,2]{0,1:T(2,128)}, u32[]{:S(2)}) copy-start(s32[16,2]{0,1:T(2,128)} %param.20) | copy-start | bytes 388
  110.9 45.6 %copy-start.19 = (pred[4,4]{1,0:T(4,128)(4,1)}, pred[4,4]{1,0:T(4,128)(4,1)S(1)}, u32[]{:S(2)}) copy-start(pred[4,4]{1,0:T(4,128)(4,1)S(1)} %iota_compare_fusion.2) | copy-start | bytes 52
  114.5 5.1 %copy-start.14 = (pred[8,128]{1,0:T(8,128)(4,1)}, pred[8,128]{1,0:T(8,128)(4,1)S(1)}, u32[]{:S(2)}) copy-start(pred[8,128]{1,0:T(8,128)(4,1)S(1)} %broadcast_in_dim.235) | copy-start | bytes 3076
  134.9 19.4 %copy-start.21 = (f32[8]{0:T(128)}, f32[8]{0:T(128)S(1)}, u32[]{:S(2)}) copy-start(f32[8]{0:T(128)S(1)} %pad.13.clone) | copy-start | bytes 100
  154.2 10.9 %copy-start.3 = (bf16[2,64,2048]{2,1,0:T(8,128)(2,1)S(1)}, bf16[2,64,2048]{2,1,0:T(8,128)(2,1)}, u32[]{:S(2)}) copy-start(bf16[2,64,2048]{2,1,0:T(8,128)(2,1)} %param.29) | copy-start | bytes 1572868
  155.4 1.1 copy-start.6
  155.4 3.5 %copy-start.10 = (f32[256]{0:T(256)}, f32[256]{0:T(256)S(1)}, u32[]{:S(2)}) copy-start(f32[256]{0:T(256)S(1)} %max.32) | copy-start | bytes 3076
  160.0 4.5 %copy-start.13 = (f32[2,2048]{1,0:T(2,128)S(1)}, f32[2,2048]{1,0:T(2,128)}, u32[]{:S(2)}) copy-start(f32[2,2048]{1,0:T(2,128)} %param.27) | copy-start | bytes 49156
  214.6 4.4 %copy-start.9 = (f32[256]{0:T(256)S(1)}, f32[256]{0:T(256)}, u32[]{:S(2)}) copy-start(f32[256]{0:T(256)} %copy-done.8) | copy-start | bytes 3076
  214.6 4.4 %copy-start.17 = (f32[16]{0:T(128)S(1)}, f32[16]{0:T(128)}, u32[]{:S(2)}) copy-start(f32[16]{0:T(128)} %copy-done.16) | copy-start | bytes 196
  216.9 15.8 %copy-start.20 = (pred[4,4]{1,0:T(4,128)(4,1)S(1)}, pred[4,4]{1,0:T(4,128)(4,1)}, u32[]{:S(2)}) copy-start(pred[4,4]{1,0:T(4,128)(4,1)} %copy-done.19) | copy-start | bytes 52
  219.0 17.1 %copy-start.15 = (pred[8,128]{1,0:T(8,128)(4,1)S(1)}, pred[8,128]{1,0:T(8,128)(4,1)}, u32[]{:S(2)}) copy-start(pred[8,128]{1,0:T(8,128)(4,1)} %copy-done.14) | copy-start | bytes 3076
  249.7 3.3 %copy-start.22 = (f32[8]{0:T(128)S(1)}, f32[8]{0:T(128)}, u32[]{:S(2)}) copy-start(f32[8]{0:T(128)} %copy-done.21) | copy-start | bytes 100
  272.4 8.3 %copy-start.4 = (bf16[2,64,2048]{2,1,0:T(8,128)(2,1)S(1)}, bf16[2,64,2048]{2,1,0:T(8,128)(2,1)}, u32[]{:S(2)}) copy-start(bf16[2,64,2048]{2,1,0:T(8,128)(2,1)} %param.29) | copy-start | bytes 1572868
  272.4 8.3 %copy-start.23 = (f32[64]{0:T(128)S(1)}, f32[64]{0:T(128)}, u32[]{:S(2)}) copy-start(f32[64]{0:T(128)} %get-tuple-element.63) | copy-start | bytes 772
  (4 other events, 3.2 us)
